TPU v7x, 32 devices: a whole 2x2x4 slice. The times are simulated.
32 devices in a mesh: dp: 8 (over z, x), tensor: 4 (over y, core).
Axes of the slice: x: 2, y: 2, z: 4, core: 2. Of those that a mesh axis runs over, the one named last changes fastest.
Arguments:
- clips: bfloat16 [16, 512, 1280], P('dp', 'tensor'), may hold values from -6 to 6
- lengths: int32 [16], P('dp'), may hold values from 1 to 512, 6144 in all
- norm1_gain: bfloat16 [1280], P('dp'), may hold values from 0.25 to 1.75
- norm1_bias: bfloat16 [1280], P('dp'), may hold values from -2 to 2
- w_query: bfloat16 [1280, 1280], P('dp', 'tensor'), may hold values from -0.25 to 0.25
- bias_query: bfloat16 [1280], P('tensor'), may hold values from -3 to 3
- w_key: bfloat16 [1280, 1280], P('dp', 'tensor'), may hold values from -0.15625 to 0.15625
- w_value: bfloat16 [1280, 1280], P('dp', 'tensor'), may hold values from -0.15625 to 0.15625
- bias_value: bfloat16 [1280], P('tensor'), may hold values from -3 to 3
- w_out: bfloat16 [1280, 1280], P('tensor', 'dp'), may hold values from -1.25 to 1.25
- bias_out: bfloat16 [1280], P('dp'), may hold values from -3 to 3
- norm2_gain: bfloat16 [1280], P('dp'), may hold values from 0.25 to 1.75
- norm2_bias: bfloat16 [1280], P('dp'), may hold values from -2 to 2
- w_up: bfloat16 [1280, 5120], P('dp', 'tensor'), may hold values from -0.15625 to 0.15625
- bias_up: bfloat16 [5120], P('tensor'), may hold values from -3 to 3
- w_down: bfloat16 [5120, 1280], P('tensor', 'dp'), may hold values from -0.078125 to 0.078125
- bias_down: bfloat16 [1280], P('dp'), may hold values from -3 to 3
- cotangent: bfloat16 [16, 512, 1280], P('dp', 'tensor'), may hold values from -6 to 6
Outputs:
- output: bfloat16 [16, 512, 1280], P('dp', 'tensor')
- clip_grad: float32 [16, 512, 1280], P('dp', 'tensor')
- norm1_gain_grad: float32 [1280], P('dp')
- norm1_bias_grad: float32 [1280], P('dp')
- w_query_grad: float32 [1280, 1280], P('dp', 'tensor')
- bias_query_grad: float32 [1280], P('tensor')
- w_key_grad: float32 [1280, 1280], P('dp', 'tensor')
- w_value_grad: float32 [1280, 1280], P('dp', 'tensor')
- bias_value_grad: float32 [1280], P('tensor')
- w_out_grad: float32 [1280, 1280], P('tensor', 'dp')
- bias_out_grad: float32 [1280], P('dp')
- norm2_gain_grad: float32 [1280], P('dp')
- norm2_bias_grad: float32 [1280], P('dp')
- w_up_grad: float32 [1280, 5120], P('dp', 'tensor')
- bias_up_grad: float32 [5120], P('tensor')
- w_down_grad: float32 [5120, 1280], P('tensor', 'dp')
- bias_down_grad: float32 [1280], P('dp')
Inputs may be any that keep to these rules, and one draw needn't show every extreme that they name: `lengths`: positions of a clip at or beyond its length are padding, whose keys are masked.
All inputs are finite; a program needn't handle non-finite values. No bound on the sum of `lengths` on one device may be relied on, other than what follows from the above.
Results may differ from a plain program's by a relative error of at most 0.014.
Values may be sent and summed in bfloat16 or wider, within the bound.
No kernel may reach another device: no remote copies, remote signals or barrier semaphores. Data moves between devices by JAX's collectives and lax.ppermute only.
A program may use at most 192 MiB of HBM per device.

v0:
```python
import jax
import jax.numpy as jnp
from jax import lax
from jax.sharding import PartitionSpec as P

HEAD_DIM = 80


norm_eps = 1e-05


def layer_norm(values, gain, shift):
    center = values - jnp.mean(values, axis=-1, keepdims=True)
    spread = jnp.mean(center * center, axis=-1, keepdims=True)
    return center * lax.rsqrt(spread + norm_eps) * gain + shift


def exact_gelu(values):
    return jax.nn.gelu(values, approximate=False)


def to_low(values):
    return values.astype(jnp.bfloat16)


def matmul(left, right):
    return jnp.dot(left, right, preferred_element_type=jnp.float32)


def matmul_left(left, right):
    return lax.dot_general(
        left, right, (((0,), (0,)), ((), ())), preferred_element_type=jnp.float32
    )


def matmul_right(left, right):
    return lax.dot_general(
        left, right, (((1,), (1,)), ((), ())), preferred_element_type=jnp.float32
    )


def score_rows(query, keys, length):
    scale = query.shape[2] ** (-0.5)
    scores = jnp.einsum("ihd,jhd->hij", query, keys, preferred_element_type=jnp.float32) * scale
    visible = lax.iota(jnp.int32, keys.shape[0]) < length
    return jnp.where(visible[None, None, :], scores, -1000000000.0)


def attend(query, keys, values, length):
    scores = score_rows(query, keys, length)
    top = jnp.max(scores, axis=-1, keepdims=True)
    expo = jnp.exp(scores - top)
    total = jnp.sum(expo, axis=-1, keepdims=True)
    probs = expo / total
    mixed = jnp.einsum("hij,jhd->ihd", to_low(probs), values, preferred_element_type=jnp.float32)
    return (to_low(mixed.reshape(mixed.shape[0], -1)), top + jnp.log(total))


def attend_back(query, keys, values, length, log_total, grad_mixed):
    scale = query.shape[2] ** (-0.5)
    probs = jnp.exp(score_rows(query, keys, length) - log_total)
    grad_heads = grad_mixed.reshape(query.shape)
    grad_probs = jnp.einsum("ihd,jhd->hij", grad_heads, values, preferred_element_type=jnp.float32)
    delta = jnp.sum(grad_probs * probs, axis=-1, keepdims=True)
    grad_scores = to_low(probs * (grad_probs - delta))
    grad_query = (
        jnp.einsum("hij,jhd->ihd", grad_scores, keys, preferred_element_type=jnp.float32) * scale
    )
    grad_keys = (
        jnp.einsum("hij,ihd->jhd", grad_scores, query, preferred_element_type=jnp.float32) * scale
    )
    grad_values = jnp.einsum(
        "hij,ihd->jhd", to_low(probs), grad_heads, preferred_element_type=jnp.float32
    )
    tokens = query.shape[0]
    joined = jnp.concatenate(
        [
            grad_query.reshape(tokens, -1),
            grad_keys.reshape(tokens, -1),
            grad_values.reshape(tokens, -1),
        ],
        axis=1,
    )
    return to_low(joined)


def attn_parts(gathered):
    gain_full, shift_full, query_full, key_full, value_full, out_full, out_bias_full = gathered
    joined = jnp.concatenate([query_full, key_full, value_full], axis=1)
    return (
        gain_full.astype(jnp.float32),
        shift_full.astype(jnp.float32),
        joined,
        out_full,
        out_bias_full.astype(jnp.float32),
    )


def mlp_parts(gathered):
    gain_full, shift_full, up_full, down_full, down_bias_full = gathered
    return (
        gain_full.astype(jnp.float32),
        shift_full.astype(jnp.float32),
        up_full,
        down_full,
        down_bias_full.astype(jnp.float32),
    )


def add_tree(first, second):
    return jax.tree.map(jnp.add, first, second)


def shards(
    clips,
    lengths,
    norm1_gain,
    norm1_bias,
    w_query,
    bias_query,
    w_key,
    w_value,
    bias_value,
    w_out,
    bias_out,
    norm2_gain,
    norm2_bias,
    w_up,
    bias_up,
    w_down,
    bias_down,
    cotangent,
):
    local_rows = clips.shape[1]
    width = w_query.shape[1]
    heads_local = width // HEAD_DIM
    attn_full = (
        lax.all_gather(norm1_gain, "dp", axis=0, tiled=True),
        lax.all_gather(norm1_bias, "dp", axis=0, tiled=True),
        lax.all_gather(w_query, "dp", axis=0, tiled=True),
        lax.all_gather(w_key, "dp", axis=0, tiled=True),
        lax.all_gather(w_value, "dp", axis=0, tiled=True),
        lax.all_gather(w_out, "dp", axis=1, tiled=True),
        lax.all_gather(bias_out, "dp", axis=0, tiled=True),
    )
    mlp_full = (
        lax.all_gather(norm2_gain, "dp", axis=0, tiled=True),
        lax.all_gather(norm2_bias, "dp", axis=0, tiled=True),
        lax.all_gather(w_up, "dp", axis=0, tiled=True),
        lax.all_gather(w_down, "dp", axis=1, tiled=True),
        lax.all_gather(bias_down, "dp", axis=0, tiled=True),
    )
    gain_one, shift_one, joined_qkv, out_full, out_bias = attn_parts(attn_full)
    gain_two, shift_two, up_full, down_full, down_bias = mlp_parts(mlp_full)
    bias_joined = jnp.concatenate(
        [
            bias_query.astype(jnp.float32),
            jnp.zeros((width,), jnp.float32),
            bias_value.astype(jnp.float32),
        ]
    )
    bias_hidden = bias_up.astype(jnp.float32)
    acc_bias_qkv = jnp.zeros((3 * width,), jnp.float32)
    acc_bias_up = jnp.zeros(bias_hidden.shape, jnp.float32)
    local_total = None
    owned_total = None
    outputs = []
    input_grads = []
    for batch_index in range(clips.shape[0]):
        rows = clips[batch_index].astype(jnp.float32)
        length = lengths[batch_index]
        normed_one = to_low(layer_norm(rows, gain_one, shift_one))
        whole_one = lax.all_gather(normed_one, "tensor", axis=0, tiled=True)
        tokens = whole_one.shape[0]
        projected = to_low(matmul(whole_one, joined_qkv) + bias_joined)
        head_shape = (tokens, heads_local, HEAD_DIM)
        query = projected[:, :width].reshape(head_shape)
        keys = projected[:, width : 2 * width].reshape(head_shape)
        values = projected[:, 2 * width :].reshape(head_shape)
        mixed, log_total = attend(query, keys, values, length)

        def attn_term(start, count, mixed=mixed):
            return matmul(mixed, out_full)

        branch_one = lax.psum_scatter(
            attn_term(jnp.int32(0), lax.axis_size("tensor") * local_rows),
            "tensor",
            scatter_dimension=0,
            tiled=True,
        )
        inner = rows + (branch_one + out_bias)
        normed_two = to_low(layer_norm(inner, gain_two, shift_two))
        whole_two = lax.all_gather(normed_two, "tensor", axis=0, tiled=True)
        hidden_pre = matmul(whole_two, up_full) + bias_hidden
        hidden = to_low(exact_gelu(hidden_pre))

        def mlp_term(start, count, hidden=hidden):
            return matmul(hidden, down_full)

        branch_two = lax.psum_scatter(
            mlp_term(jnp.int32(0), lax.axis_size("tensor") * local_rows).astype(jnp.bfloat16),
            "tensor",
            scatter_dimension=0,
            tiled=True,
        ).astype(jnp.float32)
        outputs.append(to_low(inner + (branch_two + down_bias)))
        back_attn = (
            lax.all_gather(norm1_gain, "dp", axis=0, tiled=True),
            lax.all_gather(norm1_bias, "dp", axis=0, tiled=True),
            lax.all_gather(w_query, "dp", axis=0, tiled=True),
            lax.all_gather(w_key, "dp", axis=0, tiled=True),
            lax.all_gather(w_value, "dp", axis=0, tiled=True),
            lax.all_gather(w_out, "dp", axis=1, tiled=True),
            lax.all_gather(bias_out, "dp", axis=0, tiled=True),
        )
        back_mlp = (
            lax.all_gather(norm2_gain, "dp", axis=0, tiled=True),
            lax.all_gather(norm2_bias, "dp", axis=0, tiled=True),
            lax.all_gather(w_up, "dp", axis=0, tiled=True),
            lax.all_gather(w_down, "dp", axis=1, tiled=True),
            lax.all_gather(bias_down, "dp", axis=0, tiled=True),
        )
        back_gain_one, back_shift_one, back_qkv, back_out, unused_bias_one = attn_parts(back_attn)
        back_gain_two, back_shift_two, back_up, back_down, unused_bias_two = mlp_parts(back_mlp)
        grad_top = cotangent[batch_index]
        grad_whole = lax.all_gather(grad_top, "tensor", axis=0, tiled=True)
        term_down = matmul_left(hidden, grad_whole)
        term_bias_down = jnp.sum(grad_top.astype(jnp.float32), axis=0)
        grad_hidden = matmul_right(grad_whole, back_down)
        unused_value, gelu_pull = jax.vjp(exact_gelu, hidden_pre)
        grad_pre = to_low(gelu_pull(grad_hidden)[0])
        term_up = matmul_left(whole_two, grad_pre)
        acc_bias_up = acc_bias_up + jnp.sum(grad_pre.astype(jnp.float32), axis=0)

        def mlp_back_term(start, count, grad_pre=grad_pre, back_up=back_up):
            return matmul_right(grad_pre, back_up)

        grad_normed_two = lax.psum_scatter(
            mlp_back_term(jnp.int32(0), lax.axis_size("tensor") * local_rows),
            "tensor",
            scatter_dimension=0,
            tiled=True,
        )
        unused_two, norm_two_pull = jax.vjp(layer_norm, inner, back_gain_two, back_shift_two)
        grad_inner_part, term_gain_two, term_shift_two = norm_two_pull(grad_normed_two)
        grad_inner = grad_top.astype(jnp.float32) + grad_inner_part
        grad_branch = to_low(grad_inner)
        term_bias_out = jnp.sum(grad_branch.astype(jnp.float32), axis=0)
        grad_branch_whole = lax.all_gather(grad_branch, "tensor", axis=0, tiled=True)
        term_out = matmul_left(mixed, grad_branch_whole)
        grad_mixed = to_low(matmul_right(grad_branch_whole, back_out))
        grad_qkv = attend_back(query, keys, values, length, log_total, grad_mixed)
        term_qkv = matmul_left(whole_one, grad_qkv)
        acc_bias_qkv = acc_bias_qkv + jnp.sum(grad_qkv.astype(jnp.float32), axis=0)

        def attn_back_term(start, count, grad_qkv=grad_qkv, back_qkv=back_qkv):
            return matmul_right(grad_qkv, back_qkv)

        grad_normed_one = lax.psum_scatter(
            attn_back_term(jnp.int32(0), lax.axis_size("tensor") * local_rows).astype(jnp.bfloat16),
            "tensor",
            scatter_dimension=0,
            tiled=True,
        ).astype(jnp.float32)
        unused_one, norm_one_pull = jax.vjp(layer_norm, rows, back_gain_one, back_shift_one)
        grad_rows_part, term_gain_one, term_shift_one = norm_one_pull(grad_normed_one)
        input_grads.append(grad_inner + grad_rows_part)
        terms = (
            term_gain_one,
            term_shift_one,
            term_bias_out,
            term_gain_two,
            term_shift_two,
            term_bias_down,
            term_qkv,
            term_out,
            term_up,
            term_down,
        )
        local_total = terms if local_total is None else add_tree(local_total, terms)
    small = lax.psum(
        (
            local_total[0],
            local_total[1],
            local_total[2],
            local_total[3],
            local_total[4],
            local_total[5],
        ),
        "tensor",
    )
    qkv_total = local_total[6]
    owned_total = (
        lax.psum_scatter(small[0], "dp", scatter_dimension=0, tiled=True),
        lax.psum_scatter(small[1], "dp", scatter_dimension=0, tiled=True),
        lax.psum_scatter(small[2], "dp", scatter_dimension=0, tiled=True),
        lax.psum_scatter(small[3], "dp", scatter_dimension=0, tiled=True),
        lax.psum_scatter(small[4], "dp", scatter_dimension=0, tiled=True),
        lax.psum_scatter(small[5], "dp", scatter_dimension=0, tiled=True),
        lax.psum_scatter(qkv_total[:, :width], "dp", scatter_dimension=0, tiled=True),
        lax.psum_scatter(qkv_total[:, width : 2 * width], "dp", scatter_dimension=0, tiled=True),
        lax.psum_scatter(qkv_total[:, 2 * width :], "dp", scatter_dimension=0, tiled=True),
        lax.psum_scatter(local_total[7], "dp", scatter_dimension=1, tiled=True),
        lax.psum_scatter(local_total[8], "dp", scatter_dimension=0, tiled=True),
        lax.psum_scatter(local_total[9], "dp", scatter_dimension=1, tiled=True),
    )
    bias_query_grad, bias_value_grad, bias_up_grad = lax.psum(
        (acc_bias_qkv[:width], acc_bias_qkv[2 * width :], acc_bias_up), "dp"
    )
    output = jnp.stack(outputs, axis=0)
    clip_grad = jnp.stack(input_grads, axis=0)
    return (
        output,
        clip_grad,
        owned_total[0],
        owned_total[1],
        owned_total[6],
        bias_query_grad,
        owned_total[7],
        owned_total[8],
        bias_value_grad,
        owned_total[9],
        owned_total[2],
        owned_total[3],
        owned_total[4],
        owned_total[10],
        bias_up_grad,
        owned_total[11],
        owned_total[5],
    )


def solution(mesh):
    placed = (
        P("dp", "tensor", None),
        P("dp"),
        P("dp"),
        P("dp"),
        P("dp", "tensor"),
        P("tensor"),
        P("dp", "tensor"),
        P("dp", "tensor"),
        P("tensor"),
        P("tensor", "dp"),
        P("dp"),
        P("dp"),
        P("dp"),
        P("dp", "tensor"),
        P("tensor"),
        P("tensor", "dp"),
        P("dp"),
        P("dp", "tensor", None),
    )
    return jax.shard_map(
        shards,
        mesh=mesh,
        in_specs=placed,
        out_specs=(
            P("dp", "tensor", None),
            P("dp", "tensor", None),
            P("dp"),
            P("dp"),
            P("dp", "tensor"),
            P("tensor"),
            P("dp", "tensor"),
            P("dp", "tensor"),
            P("tensor"),
            P("tensor", "dp"),
            P("dp"),
            P("dp"),
            P("dp"),
            P("dp", "tensor"),
            P("tensor"),
            P("tensor", "dp"),
            P("dp"),
        ),
        check_vma=False,
    )
```

profile of v0, /device:TPU:0, one launch (start us, length us, event | category | flops | bytes accessed | tf_op | source)
XLA Modules:
  0.0 1175.1 jit_solution(11021692708535112053)
XLA Ops:
  15.2 38.8 %all-reduce.14 = (bf16[1280]{0:T(1024)(128)(2,1)S(1)}, bf16[1280]{0:T(1024)(128)(2,1)S(1)}, bf16[1280]{0:T(1024)(128)(2,1)S(1)}, bf16[1280]{0:T(1024)(128)(2,1)S...) all-reduce(bf16[1280]{0:T(1024)(128)(2,1)S(1)} %dynamic-update-slic, ...), channel_id=1, replica_groups=mesh['dp'=8,'tensor'=4] {'dp'}, use_global_device_ids=true, to_apply=%add.1 | all-reduce | flops 7680 | bytes 30720
  60.4 33.0 %all_gather.81 = bf16[1280,320]{1,0:T(8,128)(2,1)S(1)} all-gather(bf16[160,320]{1,0:T(8,128)(2,1)S(1)} %copy-done.55), channel_id=1, replica_groups=mesh['dp'=8,'tensor'=4] {'dp'}, dimensions={0}, use_global_device_ids=true | all-gather | bytes 921600 | tf_op jit(solution)/shard_map/all_gather | solution.py:142
  93.3 32.6 %all_gather.80 = bf16[1280,320]{1,0:T(8,128)(2,1)S(1)} all-gather(bf16[160,320]{1,0:T(8,128)(2,1)S(1)} %copy-done.56), channel_id=1, replica_groups=mesh['dp'=8,'tensor'=4] {'dp'}, dimensions={0}, use_global_device_ids=true | all-gather | bytes 921600 | tf_op jit(solution)/shard_map/all_gather | solution.py:141
  126.0 35.1 %all_gather.79 = bf16[1280,320]{1,0:T(8,128)(2,1)} all-gather(bf16[160,320]{1,0:T(8,128)(2,1)S(1)} %copy-done.57), channel_id=1, replica_groups=mesh['dp'=8,'tensor'=4] {'dp'}, dimensions={0}, use_global_device_ids=true | all-gather | bytes 921600 | tf_op jit(solution)/shard_map/all_gather | solution.py:140
  162.4 31.9 %all_gather.82 = bf16[320,1280]{0,1:T(8,128)(2,1)S(1)} all-gather(bf16[320,160]{0,1:T(8,128)(2,1)S(1)} %copy-done.58), channel_id=1, replica_groups=mesh['dp'=8,'tensor'=4] {'dp'}, dimensions={1}, use_global_device_ids=true | all-gather | bytes 921600 | tf_op jit(solution)/shard_map/all_gather | solution.py:143
  194.4 3.7 add_convert_fusion.3
  204.7 3.4 add_convert_fusion.2
  214.4 21.5 %reduce-scatter.21.cloned.1.call-done = f32[128,1280]{1,0:T(8,128)} async-done(((f32[512,1280]{1,0:T(8,128)}), f32[128,1280]{1,0:T(8,128)}) %reduce-scatter.21.cloned.1.call-update) | async-done | bytes 655376 | tf_op jit(solution)/shard_map/reduce_scatter | solution.py:185
  235.9 37.3 %reduce-scatter.25.cloned.1.call-done = f32[128,1280]{1,0:T(8,128)} async-done(((f32[512,1280]{1,0:T(8,128)}), f32[128,1280]{1,0:T(8,128)}) %reduce-scatter.25.cloned.1.call-update) | async-done | bytes 655376 | tf_op jit(solution)/shard_map/reduce_scatter | solution.py:185
  279.9 14.6 %all-gather.15.cloned.1.call-done = bf16[512,1280]{1,0:T(8,128)(2,1)} async-done(((bf16[128,1280]{1,0:T(8,128)(2,1)}), bf16[512,1280]{1,0:T(8,128)(2,1)}) %all-gather.15.cloned.1.call-update) | async-done | bytes 1310736 | tf_op jit(solution)/shard_map/all_gather | solution.py:193
  294.5 10.7 multiply_convert_fusion.3
  305.2 9.3 all-gather.29.cloned.1.call-done
  314.6 63.7 %all-gather.19.cloned.1.call-done = bf16[1280,1280]{0,1:T(8,128)(2,1)} async-done(((bf16[1280,160]{0,1:T(8,128)(2,1)}), bf16[1280,1280]{0,1:T(8,128)(2,1)}) %all-gather.19.cloned.1.call-update) | async-done | bytes 3276816 | tf_op jit(solution)/shard_map/all_gather | solution.py:150
  378.3 6.5 convert_reduce_fusion.1
  385.8 3.4 fusion.107
  389.7 7.7 all-gather.23.cloned.1.call-done
  397.4 10.9 multiply_convert_fusion.2
  408.3 21.7 %all-gather.31.cloned.1.call-done = bf16[1,512,1280]{2,1,0:T(8,128)(2,1)} async-done(((bf16[1,128,1280]{2,1,0:T(8,128)(2,1)}), bf16[1,512,1280]{2,1,0:T(8,128)(2,1)}) %all-gather.31.cloned.1.call-update) | async-done | bytes 1310736 | tf_op jit(solution)/shard_map/all_gather | solution.py:226
  430.0 6.5 convert_reduce_fusion
  437.5 3.4 fusion.108
  441.0 5.3 convolution_convert_fusion.2
  446.4 5.4 convolution_convert_fusion.3
  451.9 23.9 %reduce-scatter.33.cloned.1.call-done = f32[128,1280]{1,0:T(8,128)} async-done(((f32[512,1280]{1,0:T(8,128)}), f32[128,1280]{1,0:T(8,128)}) %reduce-scatter.33.cloned.1.call-update) | async-done | bytes 655376 | tf_op jit(solution)/shard_map/reduce_scatter | solution.py:238
  477.6 27.3 %reduce-scatter.27.cloned.1.call-done = bf16[128,1280]{1,0:T(8,128)(2,1)} async-done(((bf16[512,1280]{1,0:T(8,128)(2,1)}), bf16[128,1280]{1,0:T(8,128)(2,1)}) %reduce-scatter.27.cloned.1.call-update) | async-done | bytes 327696 | tf_op jit(solution)/shard_map/reduce_scatter | solution.py:200
  505.0 29.3 %reduce-scatter.23.cloned.1.call-done = bf16[128,1280]{1,0:T(8,128)(2,1)} async-done(((bf16[512,1280]{1,0:T(8,128)(2,1)}), bf16[128,1280]{1,0:T(8,128)(2,1)}) %reduce-scatter.23.cloned.1.call-update) | async-done | bytes 327696 | tf_op jit(solution)/shard_map/reduce_scatter | solution.py:200
  534.2 2.8 fusion.89
  539.9 17.3 %all-gather.25.cloned.1.call-done = bf16[512,1280]{1,0:T(8,128)(2,1)} async-done(((bf16[128,1280]{1,0:T(8,128)(2,1)}), bf16[512,1280]{1,0:T(8,128)(2,1)}) %all-gather.25.cloned.1.call-update) | async-done | bytes 1310736 | tf_op jit(solution)/shard_map/all_gather | solution.py:249
  559.2 3.3 multiply_reduce_fusion.1
  567.5 3.2 convolution_convert_fusion.1
  570.8 6.5 all-gather.27.cloned.1.call-done
  579.3 3.3 multiply_reduce_fusion
  587.2 3.1 convolution_convert_fusion
  590.6 2.9 fusion.85
  597.1 2.8 copy.65
  600.0 2.8 copy.67
  610.4 3.8 fusion.110
  614.2 4.6 convolution_add_fusion.1
  619.2 3.7 fusion.29
  622.9 4.7 convolution_add_fusion
  632.4 3.0 reduce-scatter.35.cloned.1.call-done
  638.8 38.4 %all-reduce.12 = (f32[1280]{0:T(1024)S(1)}, f32[1280]{0:T(1024)S(1)}, f32[320]{0:T(512)}, f32[320]{0:T(512)}, f32[1280]{0:T(1024)S(1)}, /*index=5*/f32[1280]{0:T...) all-reduce(f32[1280]{0:T(1024)S(1)} %add.294, ...), channel_id=12, replica_groups=mesh['dp'=8,'tensor'=4] {'dp'}, use_global_device_ids=true, to_apply=%region_33.34.clone | all-reduce | flops 9600 | bytes 76800
  677.6 6.6 all-reduce.13
  686.1 20.2 %reduce-scatter.43.cloned.1.call-done = f32[160,320]{1,0:T(8,128)} async-done(((f32[1280,320]{1,0:T(8,128)}), f32[160,320]{1,0:T(8,128)}) %reduce-scatter.43.cloned.1.call-update) | async-done | bytes 204816
  706.2 70.5 %reduce-scatter.45.cloned.1.call-done = f32[160,320]{1,0:T(8,128)} async-done(((f32[1280,320]{1,0:T(8,128)}), f32[160,320]{1,0:T(8,128)}) %reduce-scatter.45.cloned.1.call-update) | async-done | bytes 204816
  776.7 70.1 %reduce-scatter.47.cloned.1.call-done = f32[160,320]{1,0:T(8,128)} async-done(((f32[1280,320]{1,0:T(8,128)}), f32[160,320]{1,0:T(8,128)}) %reduce-scatter.47.cloned.1.call-update) | async-done | bytes 204816
  846.8 70.4 %reduce-scatter.37.cloned.1.call-done = f32[320,160]{0,1:T(8,128)} async-done(((f32[320,1280]{0,1:T(8,128)}), f32[320,160]{0,1:T(8,128)}) %reduce-scatter.37.cloned.1.call-update) | async-done | bytes 204816 | tf_op jit(solution)/shard_map/reduce_scatter | solution.py:303
  917.2 124.7 %reduce-scatter.39.cloned.1.call-done = f32[160,1280]{1,0:T(8,128)} async-done(((f32[1280,1280]{1,0:T(8,128)}), f32[160,1280]{1,0:T(8,128)}) %reduce-scatter.39.cloned.1.call-update) | async-done | bytes 819216 | tf_op jit(solution)/shard_map/reduce_scatter | solution.py:304
  1041.9 125.1 %reduce-scatter.41.cloned.1.call-done = f32[1280,160]{0,1:T(8,128)} async-done(((f32[1280,1280]{0,1:T(8,128)}), f32[1280,160]{0,1:T(8,128)}) %reduce-scatter.41.cloned.1.call-update) | async-done | bytes 819216 | tf_op jit(solution)/shard_map/reduce_scatter | solution.py:305
  (311 shorter events, 75.2 us)
Async XLA Ops:
  8.0 52.3 %copy-start.69 = (bf16[320]{0:T(512)(128)(2,1)S(1)}, bf16[320]{0:T(512)(128)(2,1)}, u32[]{:S(2)}) copy-start(bf16[320]{0:T(512)(128)(2,1)} %param.26) | copy-start | bytes 1924
  8.0 52.3 %copy-start.70 = (bf16[320]{0:T(512)(128)(2,1)S(1)}, bf16[320]{0:T(512)(128)(2,1)}, u32[]{:S(2)}) copy-start(bf16[320]{0:T(512)(128)(2,1)} %param.23) | copy-start | bytes 1924
  8.0 52.3 %copy-start.55 = (bf16[160,320]{1,0:T(8,128)(2,1)S(1)}, bf16[160,320]{1,0:T(8,128)(2,1)}, u32[]{:S(2)}) copy-start(bf16[160,320]{1,0:T(8,128)(2,1)} %param.25) | copy-start | bytes 307204
  8.1 85.3 %copy-start.56 = (bf16[160,320]{1,0:T(8,128)(2,1)S(1)}, bf16[160,320]{1,0:T(8,128)(2,1)}, u32[]{:S(2)}) copy-start(bf16[160,320]{1,0:T(8,128)(2,1)} %param.24) | copy-start | bytes 307204
  8.1 186.3 %all-gather.13.cloned.1.call-start = ((), (), s32[]{:S(2)}) async-start(), calls=%async_computation.14 | async-start | bytes 1638400 | tf_op jit(solution)/shard_map/all_gather | solution.py:173
  54.0 72.0 %copy-start.57 = (bf16[160,320]{1,0:T(8,128)(2,1)S(1)}, bf16[160,320]{1,0:T(8,128)(2,1)}, u32[]{:S(2)}) copy-start(bf16[160,320]{1,0:T(8,128)(2,1)} %param.22) | copy-start | bytes 307204
  55.3 105.8 %copy-start.59 = (f32[128]{0:T(128)}, f32[128]{0:T(128)S(1)}, u32[]{:S(2)}) copy-start(f32[128]{0:T(128)S(1)} %get-tuple-element.159) | copy-start | bytes 1540
  55.3 105.8 %copy-start.61 = (f32[128]{0:T(128)}, f32[128]{0:T(128)S(1)}, u32[]{:S(2)}) copy-start(f32[128]{0:T(128)S(1)} %get-tuple-element.160) | copy-start | bytes 1540
  57.2 103.9 %copy-start.63 = (f32[128]{0:T(128)}, f32[128]{0:T(128)S(1)}, u32[]{:S(2)}) copy-start(f32[128]{0:T(128)S(1)} %fusion.81) | copy-start | bytes 1540
  57.2 103.9 %copy-start.65 = (f32[128]{0:T(128)}, f32[128]{0:T(128)S(1)}, u32[]{:S(2)}) copy-start(f32[128]{0:T(128)S(1)} %fusion.83) | copy-start | bytes 1540
  57.2 103.9 %copy-start.68 = (s32[2]{0:T(128)S(1)}, s32[2]{0:T(128)}, u32[]{:S(2)}) copy-start(s32[2]{0:T(128)} %param.19) | copy-start | bytes 28
  57.2 105.1 %copy-start.58 = (bf16[320,160]{0,1:T(8,128)(2,1)S(1)}, bf16[320,160]{0,1:T(8,128)(2,1)}, u32[]{:S(2)}) copy-start(bf16[320,160]{0,1:T(8,128)(2,1)} %param.27) | copy-start | bytes 307204
  59.5 145.2 %all-gather.21.cloned.1.call-start = ((), (), s32[]{:S(2)}) async-start(), calls=%async_computation.20 | async-start | bytes 1638400 | tf_op jit(solution)/shard_map/all_gather | solution.py:173
  60.3 175.6 %reduce-scatter.21.cloned.1.call-start = ((), (), s32[]{:S(2)}) async-start(), calls=%async_computation.15 | async-start | bytes 3276800 | tf_op jit(solution)/shard_map/reduce_scatter | solution.py:185
  93.3 111.3 %copy-start.44 = (bf16[1280,320]{1,0:T(8,128)(2,1)}, bf16[1280,320]{1,0:T(8,128)(2,1)S(1)}, u32[]{:S(2)}) copy-start(bf16[1280,320]{1,0:T(8,128)(2,1)S(1)} %all_gather.81) | copy-start | bytes 2457604
  126.0 68.4 %copy-start.47 = (bf16[1280,320]{1,0:T(8,128)(2,1)}, bf16[1280,320]{1,0:T(8,128)(2,1)S(1)}, u32[]{:S(2)}) copy-start(bf16[1280,320]{1,0:T(8,128)(2,1)S(1)} %all_gather.80) | copy-start | bytes 2457604
  194.3 17.0 %copy-start.6 = (bf16[320,1280]{0,1:T(8,128)(2,1)}, bf16[320,1280]{0,1:T(8,128)(2,1)S(1)}, u32[]{:S(2)}) copy-start(bf16[320,1280]{0,1:T(8,128)(2,1)S(1)} %all_gather.82) | copy-start | bytes 2457604
  203.7 69.4 %reduce-scatter.25.cloned.1.call-start = ((), (), s32[]{:S(2)}) async-start(), calls=%async_computation.21 | async-start | bytes 3276800 | tf_op jit(solution)/shard_map/reduce_scatter | solution.py:185
  211.3 61.9 %copy-start.4 = (bf16[2,128,1280]{2,1,0:T(8,128)(2,1)S(1)}, bf16[2,128,1280]{2,1,0:T(8,128)(2,1)}, u32[]{:S(2)}) copy-start(bf16[2,128,1280]{2,1,0:T(8,128)(2,1)} %param.18) | copy-start | bytes 1966084
  213.7 66.2 %all-gather.17.cloned.1.call-start = ((), (), s32[]{:S(2)}) async-start(), calls=%async_computation.17 | async-start | bytes 3686400 | tf_op jit(solution)/shard_map/all_gather | solution.py:149
  214.3 80.2 %all-gather.15.cloned.1.call-start = ((), (), s32[]{:S(2)}) async-start(), calls=%async_computation.16 | async-start | bytes 1638400 | tf_op jit(solution)/shard_map/all_gather | solution.py:193
  276.3 38.2 %all-gather.29.cloned.1.call-start = ((), (), s32[]{:S(2)}) async-start(), calls=%async_computation.33 | async-start | bytes 1638400 | tf_op jit(solution)/shard_map/all_gather | solution.py:226
  277.3 101.0 %all-gather.19.cloned.1.call-start = ((), (), s32[]{:S(2)}) async-start(), calls=%async_computation.18 | async-start | bytes 3686400 | tf_op jit(solution)/shard_map/all_gather | solution.py:150
  278.0 119.3 %all-gather.23.cloned.1.call-start = ((), (), s32[]{:S(2)}) async-start(), calls=%async_computation.22 | async-start | bytes 1638400 | tf_op jit(solution)/shard_map/all_gather | solution.py:193
  278.8 151.2 %all-gather.31.cloned.1.call-start = ((), (), s32[]{:S(2)}) async-start(), calls=%async_computation.34 | async-start | bytes 1638400 | tf_op jit(solution)/shard_map/all_gather | solution.py:226
  279.5 172.4 %reduce-scatter.29.cloned.1.call-start = ((), (), s32[]{:S(2)}) async-start(), calls=%async_computation.24 | async-start | bytes 3276800 | tf_op jit(solution)/shard_map/reduce_scatter | solution.py:238
  389.2 86.6 %reduce-scatter.33.cloned.1.call-start = ((), (), s32[]{:S(2)}) async-start(), calls=%async_computation.27 | async-start | bytes 3276800 | tf_op jit(solution)/shard_map/reduce_scatter | solution.py:238
  441.0 64.0 %reduce-scatter.27.cloned.1.call-start = ((), (), s32[]{:S(2)}) async-start(), calls=%async_computation.23 | async-start | bytes 1638400 | tf_op jit(solution)/shard_map/reduce_scatter | solution.py:200
  446.3 87.9 %reduce-scatter.23.cloned.1.call-start = ((), (), s32[]{:S(2)}) async-start(), calls=%async_computation.19 | async-start | bytes 1638400 | tf_op jit(solution)/shard_map/reduce_scatter | solution.py:200
  451.8 105.4 %all-gather.25.cloned.1.call-start = ((), (), s32[]{:S(2)}) async-start(), calls=%async_computation.25 | async-start | bytes 1638400 | tf_op jit(solution)/shard_map/all_gather | solution.py:249
  537.1 20.1 %copy-start.7 = (bf16[320,1280]{0,1:T(8,128)(2,1)S(1)}, bf16[320,1280]{0,1:T(8,128)(2,1)}, u32[]{:S(2)}) copy-start(bf16[320,1280]{0,1:T(8,128)(2,1)} %copy-done.6) | copy-start | bytes 2457604
  537.9 21.2 %copy-start.34 = (bf16[512,320]{0,1:T(8,128)(2,1)S(1)}, bf16[512,320]{0,1:T(8,128)(2,1)}, u32[]{:S(2)}) copy-start(bf16[512,320]{0,1:T(8,128)(2,1)} %copy-done.33) | copy-start | bytes 983044
  539.0 38.2 %all-gather.27.cloned.1.call-start = ((), (), s32[]{:S(2)}) async-start(), calls=%async_computation.28 | async-start | bytes 1638400 | tf_op jit(solution)/shard_map/all_gather | solution.py:249
  539.6 92.7 %reduce-scatter.31.cloned.1.call-start = ((), (), s32[]{:S(2)}) async-start(), calls=%async_computation.26 | async-start | bytes 1638400 | tf_op jit(solution)/shard_map/reduce_scatter | solution.py:259
  570.7 64.7 %reduce-scatter.35.cloned.1.call-start = ((), (), s32[]{:S(2)}) async-start(), calls=%async_computation.29 | async-start | bytes 1638400 | tf_op jit(solution)/shard_map/reduce_scatter | solution.py:259
  590.3 115.9 %reduce-scatter.43.cloned.1.call-start = ((), (), s32[]{:S(2)}) async-start(), calls=%async_computation.35 | async-start | bytes 2211840
  599.9 176.8 %reduce-scatter.45.cloned.1.call-start = ((), (), s32[]{:S(2)}) async-start(), calls=%async_computation.36 | async-start | bytes 2211840
  602.9 243.9 %reduce-scatter.47.cloned.1.call-start = ((), (), s32[]{:S(2)}) async-start(), calls=%async_computation.37 | async-start | bytes 2211840
  604.7 312.5 %reduce-scatter.37.cloned.1.call-start = ((), (), s32[]{:S(2)}) async-start(), calls=%async_computation.30 | async-start | bytes 2211840 | tf_op jit(solution)/shard_map/reduce_scatter | solution.py:303
  610.3 431.6 %reduce-scatter.39.cloned.1.call-start = ((), (), s32[]{:S(2)}) async-start(), calls=%async_computation.31 | async-start | bytes 7372800 | tf_op jit(solution)/shard_map/reduce_scatter | solution.py:304
  618.8 548.2 %reduce-scatter.41.cloned.1.call-start = ((), (), s32[]{:S(2)}) async-start(), calls=%async_computation.32 | async-start | bytes 7372800 | tf_op jit(solution)/shard_map/reduce_scatter | solution.py:305
  627.7 9.3 copy-start.72
  627.7 9.3 copy-start.64
  627.7 9.3 copy-start.66
  629.6 54.6 %copy-start.9 = (f32[128,1280]{1,0:T(8,128)S(1)}, f32[128,1280]{1,0:T(8,128)}, u32[]{:S(2)}) copy-start(f32[128,1280]{1,0:T(8,128)} %copy-done.8) | copy-start | bytes 1966084
  629.6 54.6 %copy-start.11 = (f32[128,1280]{1,0:T(8,128)S(1)}, f32[128,1280]{1,0:T(8,128)}, u32[]{:S(2)}) copy-start(f32[128,1280]{1,0:T(8,128)} %copy-done.10) | copy-start | bytes 1966084
  632.4 51.9 %copy-start.13 = (bf16[128,1280]{1,0:T(8,128)(2,1)S(1)}, bf16[128,1280]{1,0:T(8,128)(2,1)}, u32[]{:S(2)}) copy-start(bf16[128,1280]{1,0:T(8,128)(2,1)} %reduce-scatter.31.cloned.1.call-done) | copy-start | bytes 983044
  635.4 48.9 %copy-start.14 = (bf16[128,1280]{1,0:T(8,128)(2,1)S(1)}, bf16[128,1280]{1,0:T(8,128)(2,1)}, u32[]{:S(2)}) copy-start(bf16[128,1280]{1,0:T(8,128)(2,1)} %reduce-scatter.35.cloned.1.call-done) | copy-start | bytes 983044
  (54 other events, 171.3 us)
Sparse Core Ops, SparseCore 0:
  59.6 15.4 all-gather.12
  77.3 18.1 all-gather.20
  203.9 31.9 reduce-scatter.20
  238.4 34.7 reduce-scatter.24
  389.3 33.5 reduce-scatter.28
  441.1 34.6 reduce-scatter.32
  478.4 26.5 reduce-scatter.26
  507.7 26.5 reduce-scatter.22
Sparse Core Ops, SparseCore 1:
  216.4 58.7 all-gather.16
  277.2 17.3 all-gather.14
  296.5 18.0 all-gather.28
  316.8 61.5 all-gather.18
  380.5 16.8 all-gather.22
  399.0 30.9 all-gather.30
  539.1 18.0 all-gather.24
  559.2 18.0 all-gather.26
  579.7 26.4 reduce-scatter.30
  608.9 26.4 reduce-scatter.34
  639.3 66.9 reduce-scatter.42
  710.7 66.0 reduce-scatter.44
  780.7 66.1 reduce-scatter.46
  851.3 65.9 reduce-scatter.36
  921.4 120.4 reduce-scatter.38
  1046.5 120.5 reduce-scatter.40
where the time goes:
time: 1180 us
  waiting for transfers between devices  768 us (65%)
  blocking collectives  216 us (18%)
  matrix products  114 us (10%)
  other arithmetic  27.6 us (2%)
  local copies, waits for them, and re-layouts  27 us (2%)
  between operations  19.1 us (2%)
    unnamed x27, waiting for transfers between devices  165 us
    reduce_scatter x1, waiting for transfers between devices, shards(): lax.psum_scatter(local_total[9], 'dp', scatter_dimension=1, tiled=True)  125 us
    reduce_scatter x1, waiting for transfers between devices, shards(): lax.psum_scatter(local_total[8], 'dp', scatter_dimension=0, tiled=True)  125 us
    unnamed x2, blocking collectives  77.1 us
    reduce_scatter x1, waiting for transfers between devices, shards(): lax.psum_scatter(local_total[7], 'dp', scatter_dimension=1, tiled=True)  70.4 us
    all_gather x1, waiting for transfers between devices, shards(): lax.all_gather(w_down, 'dp', axis=1, tiled=True)  63.7 us
    reduce_scatter x2, waiting for transfers between devices, shards(): lax.psum_scatter(attn_term(jnp.int32(0), lax.axis_size('tensor') * local_...  58.8 us
    reduce_scatter x2, waiting for transfers between devices, shards(): lax.psum_scatter(mlp_term(jnp.int32(0), lax.axis_size('tensor') * local_r...  56.6 us
  transfers between devices with their start and end apart: 24, of which 19 were waited for; matrix products, arithmetic and copies ran while one was open for 12% of the time, Pallas kernels for 0%

commit v1 on v0

v1 whole, which is shorter than its diff:
```python
import jax
import jax.numpy as jnp
from jax import lax
from jax.sharding import PartitionSpec as P

HEAD_DIM = 80
norm_eps = 1e-05
VEC_ROWS = 16


def low(values):
    return values.astype(jnp.bfloat16)


def wide(values):
    return values.astype(jnp.float32)


def mm(left, right):
    return jnp.dot(left, right, preferred_element_type=jnp.float32)


def mm_left(left, right):
    return lax.dot_general(left, right, (((0,), (0,)), ((), ())), preferred_element_type=jnp.float32)


def mm_right(left, right):
    return lax.dot_general(left, right, (((1,), (1,)), ((), ())), preferred_element_type=jnp.float32)


def norm_parts(values):
    center = values - jnp.mean(values, axis=-1, keepdims=True)
    spread = jnp.mean(center * center, axis=-1, keepdims=True)
    inverse = lax.rsqrt(spread + norm_eps)
    return center * inverse, inverse


def norm_back(grad, xhat, inverse, gain):
    scaled = grad * gain
    first = jnp.mean(scaled, axis=-1, keepdims=True)
    second = jnp.mean(scaled * xhat, axis=-1, keepdims=True)
    return (scaled - first - xhat * second) * inverse


def gelu_pair(pre):
    half = 0.5 * (1.0 + lax.erf(pre * (0.5 ** 0.5)))
    slope = half + pre * jnp.exp(-0.5 * pre * pre) * 0.3989422804014327
    return pre * half, slope


def tensor_swap(values, mask):
    size = lax.axis_size("tensor")
    return lax.ppermute(values, "tensor", [(i, i ^ mask) for i in range(size)])


def data_swap(values, mask):
    size = lax.axis_size("dp")
    return lax.ppermute(values, "dp", [(i, i ^ mask) for i in range(size)])


def masks_of(size):
    masks = []
    while size > 1:
        size //= 2
        masks.append(size)
    return masks


def gather_blocks(shard):
    size = lax.axis_size("dp")
    held = shard[None]
    order = [0]
    for mask in masks_of(size):
        held = jnp.concatenate([held, data_swap(held, mask)], axis=0)
        order = order + [item ^ mask for item in order]
    place = [0] * size
    for position, item in enumerate(order):
        place[item] = position
    me = lax.axis_index("dp")
    table = jnp.asarray(place, jnp.int32)
    return jnp.concatenate([lax.dynamic_slice_in_dim(held, table[me ^ item], 1, axis=0) for item in range(size)], axis=0)


def scatter_blocks(blocks):
    size = lax.axis_size("dp")
    me = lax.axis_index("dp")
    held = blocks
    for mask in reversed(masks_of(size)):
        pairs = held.reshape((held.shape[0] // 2, 2) + held.shape[1:])
        bit = (me // mask) % 2
        keep = lax.dynamic_index_in_dim(pairs, bit, axis=1, keepdims=False)
        send = lax.dynamic_index_in_dim(pairs, 1 - bit, axis=1, keepdims=False)
        held = low(wide(keep) + wide(data_swap(send, mask)))
    return held[0]


def heads_of(joined, width, index):
    tokens = joined.shape[0]
    part = joined[:, index * width : (index + 1) * width]
    return part.reshape(tokens, width // HEAD_DIM, HEAD_DIM)


def attend(query, keys, values, visible):
    scale = HEAD_DIM ** (-0.5)
    scores = jnp.einsum("ihd,jhd->hij", query, keys, preferred_element_type=jnp.float32) * scale
    scores = jnp.where(visible[None, None, :], scores, -1000000000.0)
    top = jnp.max(scores, axis=-1, keepdims=True)
    expo = jnp.exp(scores - top)
    total = jnp.sum(expo, axis=-1, keepdims=True)
    probs = low(expo / total)
    mixed = jnp.einsum("hij,jhd->ihd", probs, values, preferred_element_type=jnp.float32)
    return low(mixed.reshape(mixed.shape[0], -1)), top + jnp.log(total)


def attend_back(query, keys, values, visible, log_total, grad_mixed):
    scale = HEAD_DIM ** (-0.5)
    tokens = query.shape[0]
    scores = jnp.einsum("ihd,jhd->hij", query, keys, preferred_element_type=jnp.float32) * scale
    scores = jnp.where(visible[None, None, :], scores, -1000000000.0)
    probs = jnp.exp(scores - log_total)
    grad_heads = grad_mixed.reshape(query.shape)
    grad_probs = jnp.einsum("ihd,jhd->hij", grad_heads, values, preferred_element_type=jnp.float32)
    delta = jnp.sum(grad_probs * probs, axis=-1, keepdims=True)
    grad_scores = low(probs * (grad_probs - delta))
    grad_query = jnp.einsum("hij,jhd->ihd", grad_scores, keys, preferred_element_type=jnp.float32) * scale
    grad_keys = jnp.einsum("hij,ihd->jhd", grad_scores, query, preferred_element_type=jnp.float32) * scale
    grad_values = jnp.einsum("hij,ihd->jhd", low(probs), grad_heads, preferred_element_type=jnp.float32)
    parts = [item.reshape(tokens, -1) for item in (grad_query, grad_keys, grad_values)]
    return low(jnp.concatenate(parts, axis=1))


def pick(pair, index):
    return lax.dynamic_index_in_dim(pair, index, axis=0, keepdims=False)


def order_pair(mine, other, core):
    return jnp.where(core == 0, jnp.stack([mine, other]), jnp.stack([other, mine]))


def shards(
    clips,
    lengths,
    norm1_gain,
    norm1_bias,
    w_query,
    bias_query,
    w_key,
    w_value,
    bias_value,
    w_out,
    bias_out,
    norm2_gain,
    norm2_bias,
    w_up,
    bias_up,
    w_down,
    bias_down,
    cotangent,
):
    rows = clips.shape[1]
    model = clips.shape[2]
    depth, width = w_query.shape
    hidden_width = w_up.shape[1]
    half_hidden = hidden_width // 2
    data_size = lax.axis_size("dp")
    place = lax.axis_index("tensor")
    core = place % 2

    vectors = jnp.stack([norm1_gain, norm1_bias, bias_out, norm2_gain, norm2_bias, bias_down])
    vectors = jnp.pad(vectors, ((0, VEC_ROWS - 6), (0, model - depth)))
    attn_shard = jnp.concatenate([w_query, w_key, w_value, w_out.T], axis=1)
    attn_shard = jnp.concatenate([attn_shard, vectors], axis=0)
    down_t = w_down.T
    ff_shards = [
        jnp.concatenate([w_up[:, k * half_hidden : (k + 1) * half_hidden], down_t[:, k * half_hidden : (k + 1) * half_hidden]], axis=1)
        for k in range(2)
    ]

    local_bias = jnp.zeros((VEC_ROWS, model), jnp.bfloat16)
    local_bias = local_bias.at[0, :hidden_width].set(bias_up)
    local_bias = local_bias.at[1, : 2 * width].set(jnp.concatenate([bias_query, bias_value]))
    sent = jnp.concatenate([pick(clips, 1 - core), pick(cotangent, 1 - core), local_bias], axis=0)
    got = tensor_swap(sent, 1)
    half_rows = jnp.concatenate([pick(clips, core), got[:rows], pick(cotangent, core), got[rows : 2 * rows]], axis=0)
    sib_bias = got[2 * rows :]
    other_half = tensor_swap(half_rows, 2)
    low_rows = jnp.concatenate([half_rows[: 2 * rows], other_half[: 2 * rows]], axis=0)
    cot = jnp.concatenate([half_rows[2 * rows :], other_half[2 * rows :]], axis=0)
    cot_wide = wide(cot)
    x = wide(low_rows)
    length = pick(lengths, core)
    block = place ^ lax.iota(jnp.int32, 4)
    position = (block[:, None] * rows + lax.iota(jnp.int32, rows)[None, :]).reshape(-1)
    visible = position < length

    attn_all = gather_blocks(attn_shard)
    attn_own = attn_all[:, :depth].reshape(model, model)
    vectors_full = wide(attn_all[:, depth : depth + 6, :depth].transpose(1, 0, 2).reshape(6, model))
    gain_one, shift_one, out_bias, gain_two, shift_two, down_bias = [vectors_full[k] for k in range(6)]
    attn_sib = tensor_swap(attn_own, 1)
    attn_w = (attn_own, attn_sib)
    ff_own = [gather_blocks(item).reshape(model, model) for item in ff_shards]
    ff_sib = [tensor_swap(item, 1) for item in ff_own]

    xhat_one, inverse_one = norm_parts(x)
    normed_one = low(xhat_one * gain_one + shift_one)
    biases = (local_bias, sib_bias)
    saved = []
    partial_out = None
    for k in range(2):
        bias_row = wide(biases[k][1])
        bias_joined = jnp.concatenate([bias_row[:width], jnp.zeros((width,), jnp.float32), bias_row[width : 2 * width]])
        joined = low(mm(normed_one, attn_w[k][:, : 3 * width]) + bias_joined)
        query, keys, values = [heads_of(joined, width, i) for i in range(3)]
        mixed, log_total = attend(query, keys, values, visible)
        saved.append((query, keys, values, mixed, log_total))
        term = mm_right(mixed, attn_w[k][:, 3 * width :])
        partial_out = term if partial_out is None else partial_out + term

    def both_halves(partial):
        first = tensor_swap(low(partial[2 * rows :]), 2)
        second = tensor_swap(low(partial[: 2 * rows]), 2)
        return partial + wide(jnp.concatenate([first, second], axis=0))

    def own_half(partial):
        return partial[: 2 * rows] + wide(tensor_swap(low(partial[2 * rows :]), 2))

    inner = x + (both_halves(partial_out) + out_bias)
    xhat_two, inverse_two = norm_parts(inner)
    normed_two = low(xhat_two * gain_two + shift_two)

    branch_two = None
    grad_two = None
    ff_grads = []
    bias_up_terms = [[], []]
    for k in range(2):
        sums = []
        for side, weights in enumerate((ff_own[k], ff_sib[k])):
            up, down = weights[:, :half_hidden], weights[:, half_hidden:]
            bias = wide(biases[side][0, k * half_hidden : (k + 1) * half_hidden])
            pre = mm(normed_two, up) + bias
            act, slope = gelu_pair(pre)
            hidden = low(act)
            term = mm_right(hidden, down)
            branch_two = term if branch_two is None else branch_two + term
            grad_pre = low(mm(cot, down) * slope)
            term = mm_right(grad_pre, up)
            grad_two = term if grad_two is None else grad_two + term
            bias_up_terms[side].append(jnp.sum(wide(grad_pre), axis=0))
            sums.append(jnp.concatenate([mm_left(normed_two, grad_pre), mm_left(cot, hidden)], axis=1))
        ff_grads.append(low(sums[0] + wide(tensor_swap(low(sums[1]), 1))))

    out_half = inner[: 2 * rows] + (own_half(branch_two) + down_bias)
    out_low = low(out_half)
    output = order_pair(out_low[:rows], tensor_swap(out_low[rows:], 1), core)

    ff_shard_grads = [wide(scatter_blocks(item.reshape(data_size, depth, model))) for item in ff_grads]

    grad_normed_two = both_halves(grad_two)
    grad_inner = cot_wide + norm_back(grad_normed_two, xhat_two, inverse_two, gain_two)
    grad_branch = low(grad_inner)
    own = slice(0, 2 * rows)
    v_gain_two = jnp.sum(grad_normed_two[own] * xhat_two[own], axis=0)
    v_shift_two = jnp.sum(grad_normed_two[own], axis=0)
    v_bias_out = jnp.sum(wide(grad_branch[own]), axis=0)
    v_bias_down = jnp.sum(cot_wide[own], axis=0)

    grad_one = None
    attn_grads = []
    bias_terms = []
    for k in range(2):
        query, keys, values, mixed, log_total = saved[k]
        grad_mixed = low(mm(grad_branch, attn_w[k][:, 3 * width :]))
        grad_qkv = attend_back(query, keys, values, visible, log_total, grad_mixed)
        term = mm_right(grad_qkv, attn_w[k][:, : 3 * width])
        grad_one = term if grad_one is None else grad_one + term
        sums = jnp.sum(wide(grad_qkv), axis=0)
        bias_terms.append(jnp.concatenate([sums[:width], sums[2 * width :]] + bias_up_terms[k]))
        attn_grads.append(jnp.concatenate([mm_left(normed_one, grad_qkv), mm_left(grad_branch, mixed)], axis=1))
    attn_grad = low(attn_grads[0] + wide(tensor_swap(low(attn_grads[1]), 1)))
    attn_shard_grad = wide(scatter_blocks(attn_grad.reshape(data_size, depth, model)))

    grad_normed_one = own_half(grad_one)
    v_gain_one = jnp.sum(grad_normed_one * xhat_one[own], axis=0)
    v_shift_one = jnp.sum(grad_normed_one, axis=0)
    clip_half = grad_inner[own] + norm_back(grad_normed_one, xhat_one[own], inverse_one[own], gain_one)
    clip_grad = order_pair(clip_half[:rows], tensor_swap(clip_half[rows:], 1), core)

    bias_total = bias_terms[0] + tensor_swap(bias_terms[1], 1)
    bias_total = lax.psum(bias_total, "dp")
    vector_total = jnp.stack([v_gain_one, v_shift_one, v_bias_out, v_gain_two, v_shift_two, v_bias_down])
    vector_total = lax.psum(vector_total, ("dp", "tensor"))
    vector_own = lax.dynamic_slice_in_dim(vector_total, lax.axis_index("dp") * depth, depth, axis=1)

    w_out_grad = attn_shard_grad[:, 3 * width :].T
    w_up_grad = jnp.concatenate([item[:, :half_hidden] for item in ff_shard_grads], axis=1)
    w_down_grad = jnp.concatenate([item[:, half_hidden:] for item in ff_shard_grads], axis=1).T
    return (
        output,
        clip_grad,
        vector_own[0],
        vector_own[1],
        attn_shard_grad[:, :width],
        bias_total[:width],
        attn_shard_grad[:, width : 2 * width],
        attn_shard_grad[:, 2 * width : 3 * width],
        bias_total[width : 2 * width],
        w_out_grad,
        vector_own[2],
        vector_own[3],
        vector_own[4],
        w_up_grad,
        bias_total[2 * width :],
        w_down_grad,
        vector_own[5],
    )


def solution(mesh):
    rows_spec = P("dp", "tensor", None)
    data, tensor = P("dp"), P("tensor")
    wide_spec, tall_spec = P("dp", "tensor"), P("tensor", "dp")
    placed = (
        rows_spec,
        data,
        data,
        data,
        wide_spec,
        tensor,
        wide_spec,
        wide_spec,
        tensor,
        tall_spec,
        data,
        data,
        data,
        wide_spec,
        tensor,
        tall_spec,
        data,
        rows_spec,
    )
    outs = (
        rows_spec,
        rows_spec,
        data,
        data,
        wide_spec,
        tensor,
        wide_spec,
        wide_spec,
        tensor,
        tall_spec,
        data,
        data,
        data,
        wide_spec,
        tensor,
        tall_spec,
        data,
    )
    return jax.shard_map(shards, mesh=mesh, in_specs=placed, out_specs=outs, check_vma=False)
```

time: 1180 us -> 644 us (0.55)
  waiting for transfers between devices: 768 us -> 295 us
  blocking collectives: 216 us -> 59.2 us
  starting transfers between devices: 2.59 us -> 39.5 us
  local copies, waits for them, and re-layouts: 27 us -> 63.4 us
  other arithmetic: 27.6 us -> 62.9 us
  matrix products: 114 us -> 98.8 us
    reduce_scatter x11 -> x0, waiting for transfers between devices: 463 us -> none  [the longest x1 125 us: shards(): lax.psum_scatter(local_total[9], 'dp', scatter_dimension=1, tiled=True)]
    ppermute x0 -> x35, waiting for transfers between devices: none -> 295 us  [the longest x18 242 us: data_swap(): return lax.ppermute(values, 'dp', [(i, i ^ mask) for i in range(size)])]
    unnamed x27 -> x0, waiting for transfers between devices: 165 us -> none
    all_gather x10 -> x0, waiting for transfers between devices: 141 us -> none  [the longest x1 63.7 us: shards(): lax.all_gather(w_down, 'dp', axis=1, tiled=True)]
    all_gather x4 -> x0, blocking collectives: 133 us -> none  [the longest x1 35.1 us: shards(): lax.all_gather(w_query, 'dp', axis=0, tiled=True)]
    unnamed x2 -> x0, blocking collectives: 77.1 us -> none
    psum x1 -> x2, blocking collectives: 6.62 us -> 59.2 us  [the longest x1 37.4 us: shards(): vector_total = lax.psum(vector_total, ('dp', 'tensor'))]
    ppermute x0 -> x35, starting transfers between devices: none -> 39.5 us  [the longest x18 30.4 us: data_swap(): return lax.ppermute(values, 'dp', [(i, i ^ mask) for i in range(size)])]
  transfers between devices with their start and end apart: 24 -> 35, of which waited for: 19 -> 18; matrix products, arithmetic and copies ran while one was open for 12% -> 33% of each run, Pallas kernels for 0% -> 0%
where the time goes in v1:
time: 644 us; the launch traced here: 637 us
  waiting for transfers between devices  295 us (46%)
  matrix products  98.8 us (15%)
  local copies, waits for them, and re-layouts  63.4 us (10%)
  other arithmetic  62.9 us (10%)
  blocking collectives  59.2 us (9%)
  starting transfers between devices  39.5 us (6%)
  between operations  18.1 us (3%)
    ppermute x18, waiting for transfers between devices, data_swap(): return lax.ppermute(values, 'dp', [(i, i ^ mask) for i in range(size)])  242 us
    ppermute x17, waiting for transfers between devices, tensor_swap(): return lax.ppermute(values, 'tensor', [(i, i ^ mask) for i in range(size)])  52.7 us
    psum x1, blocking collectives, shards(): vector_total = lax.psum(vector_total, ('dp', 'tensor'))  37.4 us
    dot_general x12, matrix products, mm_right(): lax.dot_general(left, right, (((1,), (1,)), ((), ())), preferred_element_...  32.6 us
    dot_general x12, matrix products, mm(): return jnp.dot(left, right, preferred_element_type=jnp.float32)  32.3 us
    ppermute x18, starting transfers between devices, data_swap(): return lax.ppermute(values, 'dp', [(i, i ^ mask) for i in range(size)])  30.4 us
    convert_element_type x14, other arithmetic, low(): return values.astype(jnp.bfloat16)  28.1 us
    dot_general x12, matrix products, mm_left(): lax.dot_general(left, right, (((0,), (0,)), ((), ())), preferred_element_...  24.2 us
  transfers between devices with their start and end apart: 35, of which 18 were waited for; matrix products, arithmetic and copies ran while one was open for 33% of the time, Pallas kernels for 0%

profile of v1, /device:TPU:0, one launch (start us, length us, event | category | flops | bytes accessed | tf_op | source)
XLA Modules:
  0.0 636.9 jit_solution(6309120423996522392)
XLA Ops:
  2.0 4.1 collective-permute-start.8
  15.4 3.0 collective-permute-start.12
  37.5 6.2 collective-permute-done.8
  43.8 17.5 %collective-permute-done.12 = bf16[1,160,1280]{2,1,0:T(8,128)(2,1)S(1)} collective-permute-done((bf16[1,160,1280]{2,1,0:T(8,128)(2,1)S(1)}, bf16[1,160,1280]{2,1,0:T(8,128)(2,1)S(1)}, u32[]{:S(2)}, u32[]{:S(2)}) %collective-permute-start.12) | collective-permute-done | bytes 409632 | tf_op jit(solution)/shard_map/ppermute | solution.py:58
  68.2 10.7 %collective-permute-done.9 = bf16[2,160,1280]{2,1,0:T(8,128)(2,1)S(1)} collective-permute-done((bf16[2,160,1280]{2,1,0:T(8,128)(2,1)S(1)}, bf16[2,160,1280]{2,1,0:T(8,128)(2,1)S(1)}, u32[]{:S(2)}, u32[]{:S(2)}) %collective-permute-start.9) | collective-permute-done | bytes 819232 | tf_op jit(solution)/shard_map/ppermute | solution.py:58
  80.7 15.8 %collective-permute-done.13 = bf16[2,160,1280]{2,1,0:T(8,128)(2,1)S(1)} collective-permute-done((bf16[2,160,1280]{2,1,0:T(8,128)(2,1)S(1)}, bf16[2,160,1280]{2,1,0:T(8,128)(2,1)S(1)}, u32[]{:S(2)}, u32[]{:S(2)}) %collective-permute-start.13) | collective-permute-done | bytes 819232 | tf_op jit(solution)/shard_map/ppermute | solution.py:58
  98.2 17.4 %collective-permute-done.3 = bf16[2,176,1280]{2,1,0:T(8,128)(2,1)S(1)} collective-permute-done((bf16[2,176,1280]{2,1,0:T(8,128)(2,1)S(1)}, bf16[2,176,1280]{2,1,0:T(8,128)(2,1)S(1)}, u32[]{:S(2)}, u32[]{:S(2)}) %collective-permute-start.3) | collective-permute-done | bytes 901152 | tf_op jit(solution)/shard_map/ppermute | solution.py:58
  126.6 26.3 %collective-permute-done.14 = bf16[4,160,1280]{2,1,0:T(8,128)(2,1)S(1)} collective-permute-done((bf16[4,160,1280]{2,1,0:T(8,128)(2,1)S(1)}, bf16[4,160,1280]{2,1,0:T(8,128)(2,1)S(1)}, u32[]{:S(2)}, u32[]{:S(2)}) %collective-permute-start.14) | collective-permute-done | bytes 1638432 | tf_op jit(solution)/shard_map/ppermute | solution.py:58
  156.5 34.0 %collective-permute-done.4 = bf16[4,176,1280]{2,1,0:T(8,128)(2,1)S(1)} collective-permute-done((bf16[4,176,1280]{2,1,0:T(8,128)(2,1)S(1)}, bf16[4,176,1280]{2,1,0:T(8,128)(2,1)S(1)}, u32[]{:S(2)}, u32[]{:S(2)}) %collective-permute-start.4) | collective-permute-done | bytes 1802272 | tf_op jit(solution)/shard_map/ppermute | solution.py:58
  196.0 3.8 add_convert_fusion.3
  206.9 3.5 add_convert_fusion.2
  213.5 3.9 fusion.174
  221.7 14.7 %collective-permute-done.7 = bf16[256,1280]{1,0:T(8,128)(2,1)} collective-permute-done((bf16[256,1280]{1,0:T(8,128)(2,1)}, bf16[256,1280]{1,0:T(8,128)(2,1)}, u32[]{:S(2)}, u32[]{:S(2)}) %collective-permute-start.7) | collective-permute-done | bytes 655392 | tf_op jit(solution)/shard_map/ppermute | solution.py:53
  236.4 13.7 %collective-permute-done.6 = bf16[256,1280]{1,0:T(8,128)(2,1)} collective-permute-done((bf16[256,1280]{1,0:T(8,128)(2,1)}, bf16[256,1280]{1,0:T(8,128)(2,1)}, u32[]{:S(2)}, u32[]{:S(2)}) %collective-permute-start.6) | collective-permute-done | bytes 655392 | tf_op jit(solution)/shard_map/ppermute | solution.py:53
  250.1 5.1 fusion.156
  268.2 3.2 fusion.55
  279.6 3.1 convert_reduce_fusion.5
  299.3 2.8 convolution_add_fusion.2
  312.6 2.8 fusion.153
  315.4 2.9 fusion.176
  318.3 5.3 collective-permute-done.19
  323.6 12.4 %collective-permute-done.18 = bf16[256,1280]{1,0:T(8,128)(2,1)S(1)} collective-permute-done((bf16[256,1280]{1,0:T(8,128)(2,1)S(1)}, bf16[256,1280]{1,0:T(8,128)(2,1)S(1)}, u32[]{:S(2)}, u32[]{:S(2)}) %collective-permute-start.18) | collective-permute-done | bytes 655392 | tf_op jit(solution)/shard_map/ppermute | solution.py:53
  356.2 3.1 convolution_convert_fusion
  361.5 3.8 fusion.16
  365.3 3.3 convolution_add_fusion.7
  372.0 4.0 pad_maximum_fusion.3
  376.1 3.9 fusion.150
  381.9 6.6 %collective-permute-done.20 = bf16[256,1280]{1,0:T(8,128)(2,1)} collective-permute-done((bf16[256,1280]{1,0:T(8,128)(2,1)}, bf16[256,1280]{1,0:T(8,128)(2,1)}, u32[]{:S(2)}, u32[]{:S(2)}) %collective-permute-start.20) | collective-permute-done | bytes 655392 | tf_op jit(solution)/shard_map/ppermute | solution.py:53
  393.7 21.8 %psum.15 = f32[1920]{0:T(1024)S(1)} all-reduce(f32[1920]{0:T(1024)S(1)} %add.584), channel_id=1, replica_groups=mesh['dp'=8,'tensor'=4] {'dp'}, use_global_device_ids=true, to_apply=%region_27.28 | all-reduce | flops 1920 | bytes 15360 | tf_op jit(solution)/shard_map/psum | solution.py:290
  419.0 37.4 %psum.14 = f32[6,1280]{1,0:T(8,128)S(1)} all-reduce(f32[6,1280]{1,0:T(8,128)S(1)} %stack.91), channel_id=1, replica_groups=mesh['dp'=8,'tensor'=4] {'dp','tensor'}, use_global_device_ids=true, to_apply=%region_20.21 | all-reduce | flops 7680 | bytes 61440 | tf_op jit(solution)/shard_map/psum | solution.py:292
  457.1 3.0 maximum_select_fusion
  460.1 5.4 fusion.2
  465.5 4.0 copy.56
  473.0 5.4 fusion.1
  478.4 5.7 copy.55
  484.1 2.9 dynamic-slice_bitcast_fusion.1
  488.1 5.8 fusion
  494.0 5.6 copy.54
  502.0 8.0 %collective-permute-done.32 = bf16[4,160,1280]{2,1,0:T(8,128)(2,1)} collective-permute-done((bf16[4,160,1280]{2,1,0:T(8,128)(2,1)}, bf16[4,160,1280]{2,1,0:T(8,128)(2,1)}, u32[]{:S(2)}, u32[]{:S(2)}) %collective-permute-start.32) | collective-permute-done | bytes 1638432 | tf_op jit(solution)/shard_map/ppermute | solution.py:58
  511.9 2.9 collective-permute-start.33
  514.8 30.3 %collective-permute-done.28 = bf16[4,160,1280]{2,1,0:T(8,128)(2,1)} collective-permute-done((bf16[4,160,1280]{2,1,0:T(8,128)(2,1)}, bf16[4,160,1280]{2,1,0:T(8,128)(2,1)}, u32[]{:S(2)}, u32[]{:S(2)}) %collective-permute-start.28) | collective-permute-done | bytes 1638432 | tf_op jit(solution)/shard_map/ppermute | solution.py:58
  547.1 2.9 collective-permute-start.29
  550.0 28.0 %collective-permute-done.23 = bf16[4,160,1280]{2,1,0:T(8,128)(2,1)S(1)} collective-permute-done((bf16[4,160,1280]{2,1,0:T(8,128)(2,1)S(1)}, bf16[4,160,1280]{2,1,0:T(8,128)(2,1)S(1)}, u32[]{:S(2)}, u32[]{:S(2)}) %collective-permute-start.23) | collective-permute-done | bytes 1638432 | tf_op jit(solution)/shard_map/ppermute | solution.py:58
  578.5 2.9 collective-permute-start.24
  582.1 2.9 collective-permute-start.30
  585.0 24.0 %collective-permute-done.34 = bf16[1,160,1280]{2,1,0:T(8,128)(2,1)S(1)} collective-permute-done((bf16[1,160,1280]{2,1,0:T(8,128)(2,1)S(1)}, bf16[1,160,1280]{2,1,0:T(8,128)(2,1)S(1)}, u32[]{:S(2)}, u32[]{:S(2)}) %collective-permute-start.34) | collective-permute-done | bytes 409632 | tf_op jit(solution)/shard_map/ppermute | solution.py:58
  609.1 14.6 %collective-permute-done.30 = bf16[1,160,1280]{2,1,0:T(8,128)(2,1)S(1)} collective-permute-done((bf16[1,160,1280]{2,1,0:T(8,128)(2,1)S(1)}, bf16[1,160,1280]{2,1,0:T(8,128)(2,1)S(1)}, u32[]{:S(2)}, u32[]{:S(2)}) %collective-permute-start.30) | collective-permute-done | bytes 409632 | tf_op jit(solution)/shard_map/ppermute | solution.py:58
  626.1 9.5 %collective-permute-done.25 = bf16[1,160,1280]{2,1,0:T(8,128)(2,1)S(1)} collective-permute-done((bf16[1,160,1280]{2,1,0:T(8,128)(2,1)S(1)}, bf16[1,160,1280]{2,1,0:T(8,128)(2,1)S(1)}, u32[]{:S(2)}, u32[]{:S(2)}) %collective-permute-start.25) | collective-permute-done | bytes 409632 | tf_op jit(solution)/shard_map/ppermute | solution.py:58
  (390 shorter events, 159.1 us)
Async XLA Ops:
  2.0 41.6 %collective-permute-start.8 = (bf16[1,160,1280]{2,1,0:T(8,128)(2,1)S(1)}, bf16[1,160,1280]{2,1,0:T(8,128)(2,1)S(1)}, u32[]{:S(2)}, u32[]{:S(2)}) collective-permute-start(bf16[1,160,1280]{2,1,0:T(8,128)(2,1)S(1)} %maximum_bitcast_fusion.1), channel_id=1, source_target_pairs={{0,16},{4,20},{8,24},{12,28},{16,0},{20,4},{24,8},{28,12},{1,17},{... | collective-permute-start | bytes 1228808 | tf_op jit(solution)/shard_map/ppermute | solution.py:58
  11.4 104.2 %copy-start.22 = (bf16[1,176,1280]{2,1,0:T(8,128)(2,1)}, bf16[1,176,1280]{2,1,0:T(8,128)(2,1)S(1)}, u32[]{:S(2)}) copy-start(bf16[1,176,1280]{2,1,0:T(8,128)(2,1)S(1)} %fusion.136) | copy-start | bytes 1351684
  11.5 50.7 %collective-permute-start.2 = (bf16[1,176,1280]{2,1,0:T(8,128)(2,1)S(1)}, bf16[1,176,1280]{2,1,0:T(8,128)(2,1)S(1)}, u32[]{:S(2)}, u32[]{:S(2)}) collective-permute-start(bf16[1,176,1280]{2,1,0:T(8,128)(2,1)S(1)} %fusion.136), channel_id=1, source_target_pairs={{0,16},{4,20},{8,24},{12,28},{16,0},{20,4},{24,8},{28,12},{1,17},{... | collective-permute-start | bytes 1351688 | tf_op jit(solution)/shard_map/ppermute | solution.py:58
  12.8 106.1 %copy-start.32 = (bf16[128,1280]{1,0:T(8,128)(2,1)}, bf16[128,1280]{1,0:T(8,128)(2,1)S(1)}, u32[]{:S(2)}) copy-start(bf16[128,1280]{1,0:T(8,128)(2,1)S(1)} %get-tuple-element.99) | copy-start | bytes 983044
  14.1 103.8 %copy-start.18 = (bf16[128,1280]{1,0:T(8,128)(2,1)}, bf16[128,1280]{1,0:T(8,128)(2,1)S(1)}, u32[]{:S(2)}) copy-start(bf16[128,1280]{1,0:T(8,128)(2,1)S(1)} %get-tuple-element.97) | copy-start | bytes 983044
  15.3 48.4 %collective-permute-start = (bf16[272,1280]{1,0:T(8,128)(2,1)}, bf16[272,1280]{1,0:T(8,128)(2,1)}, u32[]{:S(2)}, u32[]{:S(2)}) collective-permute-start(bf16[272,1280]{1,0:T(8,128)(2,1)} %pad_maximum_fusion.19), channel_id=1, source_target_pairs={{0,1},{1,0},{2,3},{3,2},{4,5},{5,4},{6,7},{7,6},{8,9},{9,8},{10,11... | collective-permute-start | bytes 2088968 | tf_op jit(solution)/shard_map/ppermute | solution.py:53
  15.3 81.1 %copy-start.25 = (bf16[1,160,1280]{2,1,0:T(8,128)(2,1)}, bf16[1,160,1280]{2,1,0:T(8,128)(2,1)S(1)}, u32[]{:S(2)}) copy-start(bf16[1,160,1280]{2,1,0:T(8,128)(2,1)S(1)} %maximum_bitcast_fusion.2) | copy-start | bytes 1228804
  15.4 46.0 %collective-permute-start.12 = (bf16[1,160,1280]{2,1,0:T(8,128)(2,1)S(1)}, bf16[1,160,1280]{2,1,0:T(8,128)(2,1)S(1)}, u32[]{:S(2)}, u32[]{:S(2)}) collective-permute-start(bf16[1,160,1280]{2,1,0:T(8,128)(2,1)S(1)} %maximum_bitcast_fusion.2), channel_id=1, source_target_pairs={{0,16},{4,20},{8,24},{12,28},{16,0},{20,4},{24,8},{28,12},{1,17},{... | collective-permute-start | bytes 1228808 | tf_op jit(solution)/shard_map/ppermute | solution.py:58
  43.7 35.2 %collective-permute-start.9 = (bf16[2,160,1280]{2,1,0:T(8,128)(2,1)S(1)}, bf16[2,160,1280]{2,1,0:T(8,128)(2,1)S(1)}, u32[]{:S(2)}, u32[]{:S(2)}) collective-permute-start(bf16[2,160,1280]{2,1,0:T(8,128)(2,1)S(1)} %pad_maximum_fusion.16), channel_id=1, source_target_pairs={{0,8},{4,12},{8,0},{12,4},{16,24},{20,28},{24,16},{28,20},{1,9},{5... | collective-permute-start | bytes 2457608 | tf_op jit(solution)/shard_map/ppermute | solution.py:58
  61.4 35.1 %copy-start.38 = (bf16[1,160,1280]{2,1,0:T(8,128)(2,1)}, bf16[1,160,1280]{2,1,0:T(8,128)(2,1)S(1)}, u32[]{:S(2)}) copy-start(bf16[1,160,1280]{2,1,0:T(8,128)(2,1)S(1)} %collective-permute-done.12) | copy-start | bytes 1228804
  61.4 35.0 %collective-permute-start.13 = (bf16[2,160,1280]{2,1,0:T(8,128)(2,1)S(1)}, bf16[2,160,1280]{2,1,0:T(8,128)(2,1)S(1)}, u32[]{:S(2)}, u32[]{:S(2)}) collective-permute-start(bf16[2,160,1280]{2,1,0:T(8,128)(2,1)S(1)} %pad_maximum_fusion.17), channel_id=1, source_target_pairs={{0,8},{4,12},{8,0},{12,4},{16,24},{20,28},{24,16},{28,20},{1,9},{5... | collective-permute-start | bytes 2457608 | tf_op jit(solution)/shard_map/ppermute | solution.py:58
  62.2 53.5 %copy-start.36 = (bf16[1,176,1280]{2,1,0:T(8,128)(2,1)}, bf16[1,176,1280]{2,1,0:T(8,128)(2,1)S(1)}, u32[]{:S(2)}) copy-start(bf16[1,176,1280]{2,1,0:T(8,128)(2,1)S(1)} %collective-permute-done.2) | copy-start | bytes 1351684
  62.3 53.4 %collective-permute-start.3 = (bf16[2,176,1280]{2,1,0:T(8,128)(2,1)S(1)}, bf16[2,176,1280]{2,1,0:T(8,128)(2,1)S(1)}, u32[]{:S(2)}, u32[]{:S(2)}) collective-permute-start(bf16[2,176,1280]{2,1,0:T(8,128)(2,1)S(1)} %pad_maximum_fusion.15), channel_id=1, source_target_pairs={{0,8},{4,12},{8,0},{12,4},{16,24},{20,28},{24,16},{28,20},{1,9},{5... | collective-permute-start | bytes 2703368 | tf_op jit(solution)/shard_map/ppermute | solution.py:58
  64.8 53.0 %copy-start.14 = (bf16[128,1280]{1,0:T(8,128)(2,1)}, bf16[128,1280]{1,0:T(8,128)(2,1)S(1)}, u32[]{:S(2)}) copy-start(bf16[128,1280]{1,0:T(8,128)(2,1)S(1)} %get-tuple-element.93) | copy-start | bytes 983044
  64.8 54.1 %copy-start.30 = (bf16[128,1280]{1,0:T(8,128)(2,1)}, bf16[128,1280]{1,0:T(8,128)(2,1)S(1)}, u32[]{:S(2)}) copy-start(bf16[128,1280]{1,0:T(8,128)(2,1)S(1)} %get-tuple-element.94) | copy-start | bytes 983044
  64.9 52.5 %collective-permute-start.1 = (bf16[512,1280]{1,0:T(8,128)(2,1)S(1)}, bf16[512,1280]{1,0:T(8,128)(2,1)S(1)}, u32[]{:S(2)}, u32[]{:S(2)}) collective-permute-start(bf16[512,1280]{1,0:T(8,128)(2,1)S(1)} %pad_maximum_fusion.9), channel_id=1, source_target_pairs={{0,2},{1,3},{2,0},{3,1},{4,6},{5,7},{6,4},{7,5},{8,10},{9,11},{10,... | collective-permute-start | bytes 3932168 | tf_op jit(solution)/shard_map/ppermute | solution.py:53
  79.1 40.7 %collective-permute-start.10 = (bf16[4,160,1280]{2,1,0:T(8,128)(2,1)S(1)}, bf16[4,160,1280]{2,1,0:T(8,128)(2,1)S(1)}, u32[]{:S(2)}, u32[]{:S(2)}) collective-permute-start(bf16[4,160,1280]{2,1,0:T(8,128)(2,1)S(1)} %pad_maximum_fusion.7), channel_id=1, source_target_pairs={{0,4},{4,0},{8,12},{12,8},{16,20},{20,16},{24,28},{28,24},{1,5},{5... | collective-permute-start | bytes 4915208 | tf_op jit(solution)/shard_map/ppermute | solution.py:58
  96.6 56.3 %collective-permute-start.14 = (bf16[4,160,1280]{2,1,0:T(8,128)(2,1)S(1)}, bf16[4,160,1280]{2,1,0:T(8,128)(2,1)S(1)}, u32[]{:S(2)}, u32[]{:S(2)}) collective-permute-start(bf16[4,160,1280]{2,1,0:T(8,128)(2,1)S(1)} %pad_maximum_fusion.8), channel_id=1, source_target_pairs={{0,4},{4,0},{8,12},{12,8},{16,20},{20,16},{24,28},{28,24},{1,5},{5... | collective-permute-start | bytes 4915208 | tf_op jit(solution)/shard_map/ppermute | solution.py:58
  115.9 74.6 %collective-permute-start.4 = (bf16[4,176,1280]{2,1,0:T(8,128)(2,1)S(1)}, bf16[4,176,1280]{2,1,0:T(8,128)(2,1)S(1)}, u32[]{:S(2)}, u32[]{:S(2)}) collective-permute-start(bf16[4,176,1280]{2,1,0:T(8,128)(2,1)S(1)} %pad_maximum_fusion.6), channel_id=1, source_target_pairs={{0,4},{4,0},{8,12},{12,8},{16,20},{20,16},{24,28},{28,24},{1,5},{5... | collective-permute-start | bytes 5406728 | tf_op jit(solution)/shard_map/ppermute | solution.py:58
  118.9 257.1 %copy-start.69 = (f32[512]{0:T(512)}, f32[512]{0:T(512)S(1)}, u32[]{:S(2)}) copy-start(f32[512]{0:T(512)S(1)} %add_rsqrt_fusion.1) | copy-start | bytes 6148
  126.6 129.5 %collective-permute-start.11 = (bf16[1280,1280]{1,0:T(8,128)(2,1)}, bf16[1280,1280]{1,0:T(8,128)(2,1)}, u32[]{:S(2)}, u32[]{:S(2)}) collective-permute-start(bf16[1280,1280]{1,0:T(8,128)(2,1)} %bitcast.30), channel_id=1, source_target_pairs={{0,1},{1,0},{2,3},{3,2},{4,5},{5,4},{6,7},{7,6},{8,9},{9,8},{10,11... | collective-permute-start | bytes 9830408 | tf_op jit(solution)/shard_map/ppermute | solution.py:53
  153.3 37.2 %copy-start.23 = (bf16[1,176,1280]{2,1,0:T(8,128)(2,1)S(1)}, bf16[1,176,1280]{2,1,0:T(8,128)(2,1)}, u32[]{:S(2)}) copy-start(bf16[1,176,1280]{2,1,0:T(8,128)(2,1)} %copy-done.22) | copy-start | bytes 1351684
  153.3 37.2 %copy-start.37 = (bf16[1,176,1280]{2,1,0:T(8,128)(2,1)S(1)}, bf16[1,176,1280]{2,1,0:T(8,128)(2,1)}, u32[]{:S(2)}) copy-start(bf16[1,176,1280]{2,1,0:T(8,128)(2,1)} %copy-done.36) | copy-start | bytes 1351684
  193.4 13.5 %collective-permute-start.5 = (bf16[1280,1280]{1,0:T(8,128)(2,1)}, bf16[1280,1280]{1,0:T(8,128)(2,1)}, u32[]{:S(2)}, u32[]{:S(2)}) collective-permute-start(bf16[1280,1280]{1,0:T(8,128)(2,1)} %bitcast.15), channel_id=1, source_target_pairs={{0,1},{1,0},{2,3},{3,2},{4,5},{5,4},{6,7},{7,6},{8,9},{9,8},{10,11... | collective-permute-start | bytes 9830408 | tf_op jit(solution)/shard_map/ppermute | solution.py:53
  218.6 17.8 %collective-permute-start.7 = (bf16[256,1280]{1,0:T(8,128)(2,1)}, bf16[256,1280]{1,0:T(8,128)(2,1)}, u32[]{:S(2)}, u32[]{:S(2)}) collective-permute-start(bf16[256,1280]{1,0:T(8,128)(2,1)} %get-tuple-element.78), channel_id=1, source_target_pairs={{0,2},{1,3},{2,0},{3,1},{4,6},{5,7},{6,4},{7,5},{8,10},{9,11},{10,... | collective-permute-start | bytes 1966088 | tf_op jit(solution)/shard_map/ppermute | solution.py:53
  220.2 29.9 %collective-permute-start.6 = (bf16[256,1280]{1,0:T(8,128)(2,1)}, bf16[256,1280]{1,0:T(8,128)(2,1)}, u32[]{:S(2)}, u32[]{:S(2)}) collective-permute-start(bf16[256,1280]{1,0:T(8,128)(2,1)} %get-tuple-element.77), channel_id=1, source_target_pairs={{0,2},{1,3},{2,0},{3,1},{4,6},{5,7},{6,4},{7,5},{8,10},{9,11},{10,... | collective-permute-start | bytes 1966088 | tf_op jit(solution)/shard_map/ppermute | solution.py:53
  221.4 61.2 %collective-permute-start.15 = (bf16[1280,1280]{1,0:T(8,128)(2,1)}, bf16[1280,1280]{1,0:T(8,128)(2,1)S(1)}, u32[]{:S(2)}, u32[]{:S(2)}) collective-permute-start(bf16[1280,1280]{1,0:T(8,128)(2,1)} %bitcast.32), channel_id=1, source_target_pairs={{0,1},{1,0},{2,3},{3,2},{4,5},{5,4},{6,7},{7,6},{8,9},{9,8},{10,11... | collective-permute-start | bytes 9830408 | tf_op jit(solution)/shard_map/ppermute | solution.py:53
  287.4 71.9 %collective-permute-start.16 = (bf16[256,1280]{1,0:T(8,128)(2,1)}, bf16[256,1280]{1,0:T(8,128)(2,1)}, u32[]{:S(2)}, u32[]{:S(2)}) collective-permute-start(bf16[256,1280]{1,0:T(8,128)(2,1)} %slice.625), channel_id=1, source_target_pairs={{0,2},{1,3},{2,0},{3,1},{4,6},{5,7},{6,4},{7,5},{8,10},{9,11},{10,... | collective-permute-start | bytes 1966088 | tf_op jit(solution)/shard_map/ppermute | solution.py:53
  305.9 17.7 %collective-permute-start.19 = (bf16[256,1280]{1,0:T(8,128)(2,1)S(1)}, bf16[256,1280]{1,0:T(8,128)(2,1)S(1)}, u32[]{:S(2)}, u32[]{:S(2)}) collective-permute-start(bf16[256,1280]{1,0:T(8,128)(2,1)S(1)} %get-tuple-element.74), channel_id=1, source_target_pairs={{0,2},{1,3},{2,0},{3,1},{4,6},{5,7},{6,4},{7,5},{8,10},{9,11},{10,... | collective-permute-start | bytes 1966088 | tf_op jit(solution)/shard_map/ppermute | solution.py:53
  306.4 29.6 %collective-permute-start.18 = (bf16[256,1280]{1,0:T(8,128)(2,1)S(1)}, bf16[256,1280]{1,0:T(8,128)(2,1)S(1)}, u32[]{:S(2)}, u32[]{:S(2)}) collective-permute-start(bf16[256,1280]{1,0:T(8,128)(2,1)S(1)} %get-tuple-element.73), channel_id=1, source_target_pairs={{0,2},{1,3},{2,0},{3,1},{4,6},{5,7},{6,4},{7,5},{8,10},{9,11},{10,... | collective-permute-start | bytes 1966088 | tf_op jit(solution)/shard_map/ppermute | solution.py:53
  309.9 150.2 %collective-permute-start.31 = (bf16[1280,1280]{0,1:T(8,128)(2,1)}, bf16[1280,1280]{0,1:T(8,128)(2,1)}, u32[]{:S(2)}, u32[]{:S(2)}) collective-permute-start(bf16[1280,1280]{0,1:T(8,128)(2,1)} %pad_maximum_fusion.5), channel_id=1, source_target_pairs={{0,1},{1,0},{2,3},{3,2},{4,5},{5,4},{6,7},{7,6},{8,9},{9,8},{10,11... | collective-permute-start | bytes 9830408 | tf_op jit(solution)/shard_map/ppermute | solution.py:53
  312.1 160.9 %collective-permute-start.27 = (bf16[1280,1280]{0,1:T(8,128)(2,1)}, bf16[1280,1280]{0,1:T(8,128)(2,1)}, u32[]{:S(2)}, u32[]{:S(2)}) collective-permute-start(bf16[1280,1280]{0,1:T(8,128)(2,1)} %pad_maximum_fusion.4), channel_id=1, source_target_pairs={{0,1},{1,0},{2,3},{3,2},{4,5},{5,4},{6,7},{7,6},{8,9},{9,8},{10,11... | collective-permute-start | bytes 9830408 | tf_op jit(solution)/shard_map/ppermute | solution.py:53
  361.5 55.2 %collective-permute-start.17 = (bf16[128,1280]{1,0:T(8,128)(2,1)}, bf16[128,1280]{1,0:T(8,128)(2,1)}, u32[]{:S(2)}, u32[]{:S(2)}) collective-permute-start(bf16[128,1280]{1,0:T(8,128)(2,1)} %get-tuple-element.96), channel_id=1, source_target_pairs={{0,1},{1,0},{2,3},{3,2},{4,5},{5,4},{6,7},{7,6},{8,9},{9,8},{10,11... | collective-permute-start | bytes 983048 | tf_op jit(solution)/shard_map/ppermute | solution.py:53
  371.1 17.4 %collective-permute-start.20 = (bf16[256,1280]{1,0:T(8,128)(2,1)}, bf16[256,1280]{1,0:T(8,128)(2,1)}, u32[]{:S(2)}, u32[]{:S(2)}) collective-permute-start(bf16[256,1280]{1,0:T(8,128)(2,1)} %slice.624), channel_id=1, source_target_pairs={{0,2},{1,3},{2,0},{3,1},{4,6},{5,7},{6,4},{7,5},{8,10},{9,11},{10,... | collective-permute-start | bytes 1966088 | tf_op jit(solution)/shard_map/ppermute | solution.py:53
  371.7 21.5 %collective-permute-start.26 = (f32[1920]{0:T(1024)S(1)}, f32[1920]{0:T(1024)S(1)}, u32[]{:S(2)}, u32[]{:S(2)}) collective-permute-start(f32[1920]{0:T(1024)S(1)} %concatenate.160), channel_id=1, source_target_pairs={{0,1},{1,0},{2,3},{3,2},{4,5},{5,4},{6,7},{7,6},{8,9},{9,8},{10,11... | collective-permute-start | bytes 23048 | tf_op jit(solution)/shard_map/ppermute | solution.py:53
  392.9 64.2 %collective-permute-start.21 = (f32[128,1280]{1,0:T(8,128)}, f32[128,1280]{1,0:T(8,128)}, u32[]{:S(2)}, u32[]{:S(2)}) collective-permute-start(f32[128,1280]{1,0:T(8,128)} %get-tuple-element.71), channel_id=1, source_target_pairs={{0,1},{1,0},{2,3},{3,2},{4,5},{5,4},{6,7},{7,6},{8,9},{9,8},{10,11... | collective-permute-start | bytes 1966088 | tf_op jit(solution)/shard_map/ppermute | solution.py:53
  393.2 95.0 %collective-permute-start.22 = (bf16[1280,1280]{0,1:T(8,128)(2,1)}, bf16[1280,1280]{0,1:T(8,128)(2,1)}, u32[]{:S(2)}, u32[]{:S(2)}) collective-permute-start(bf16[1280,1280]{0,1:T(8,128)(2,1)} %pad_maximum_fusion.3), channel_id=1, source_target_pairs={{0,1},{1,0},{2,3},{3,2},{4,5},{5,4},{6,7},{7,6},{8,9},{9,8},{10,11... | collective-permute-start | bytes 9830408 | tf_op jit(solution)/shard_map/ppermute | solution.py:53
  470.8 39.2 %collective-permute-start.32 = (bf16[4,160,1280]{2,1,0:T(8,128)(2,1)}, bf16[4,160,1280]{2,1,0:T(8,128)(2,1)}, u32[]{:S(2)}, u32[]{:S(2)}) collective-permute-start(bf16[4,160,1280]{2,1,0:T(8,128)(2,1)} %dynamic-slice_bitcast_fusion), channel_id=1, source_target_pairs={{0,4},{4,0},{8,12},{12,8},{16,20},{20,16},{24,28},{28,24},{1,5},{5... | collective-permute-start | bytes 4915208 | tf_op jit(solution)/shard_map/ppermute | solution.py:58
  486.9 58.2 %collective-permute-start.28 = (bf16[4,160,1280]{2,1,0:T(8,128)(2,1)}, bf16[4,160,1280]{2,1,0:T(8,128)(2,1)}, u32[]{:S(2)}, u32[]{:S(2)}) collective-permute-start(bf16[4,160,1280]{2,1,0:T(8,128)(2,1)} %dynamic-slice_bitcast_fusion.1), channel_id=1, source_target_pairs={{0,4},{4,0},{8,12},{12,8},{16,20},{20,16},{24,28},{28,24},{1,5},{5... | collective-permute-start | bytes 4915208 | tf_op jit(solution)/shard_map/ppermute | solution.py:58
  501.2 44.0 %copy-start.7 = (bf16[1280,1280]{1,0:T(8,128)(2,1)S(1)}, bf16[1280,1280]{1,0:T(8,128)(2,1)}, u32[]{:S(2)}) copy-start(bf16[1280,1280]{1,0:T(8,128)(2,1)} %copy.55) | copy-start | bytes 9830404
  501.2 76.8 %collective-permute-start.23 = (bf16[4,160,1280]{2,1,0:T(8,128)(2,1)S(1)}, bf16[4,160,1280]{2,1,0:T(8,128)(2,1)S(1)}, u32[]{:S(2)}, u32[]{:S(2)}) collective-permute-start(bf16[4,160,1280]{2,1,0:T(8,128)(2,1)S(1)} %dynamic-slice_bitcast_fusion.2), channel_id=1, source_target_pairs={{0,4},{4,0},{8,12},{12,8},{16,20},{20,16},{24,28},{28,24},{1,5},{5... | collective-permute-start | bytes 4915208 | tf_op jit(solution)/shard_map/ppermute | solution.py:58
  511.9 66.1 %copy-start.8 = (bf16[1280,1280]{1,0:T(8,128)(2,1)S(1)}, bf16[1280,1280]{1,0:T(8,128)(2,1)}, u32[]{:S(2)}) copy-start(bf16[1280,1280]{1,0:T(8,128)(2,1)} %copy.54) | copy-start | bytes 9830404
  511.9 69.5 %collective-permute-start.33 = (bf16[2,160,1280]{2,1,0:T(8,128)(2,1)S(1)}, bf16[2,160,1280]{2,1,0:T(8,128)(2,1)S(1)}, u32[]{:S(2)}, u32[]{:S(2)}) collective-permute-start(bf16[2,160,1280]{2,1,0:T(8,128)(2,1)S(1)} %dynamic-slice_bitcast_fusion.3), channel_id=1, source_target_pairs={{0,8},{4,12},{8,0},{12,4},{16,24},{20,28},{24,16},{28,20},{1,9},{5... | collective-permute-start | bytes 2457608 | tf_op jit(solution)/shard_map/ppermute | solution.py:58
  547.1 34.8 %collective-permute-start.29 = (bf16[2,160,1280]{2,1,0:T(8,128)(2,1)S(1)}, bf16[2,160,1280]{2,1,0:T(8,128)(2,1)S(1)}, u32[]{:S(2)}, u32[]{:S(2)}) collective-permute-start(bf16[2,160,1280]{2,1,0:T(8,128)(2,1)S(1)} %dynamic-slice_bitcast_fusion.4), channel_id=1, source_target_pairs={{0,8},{4,12},{8,0},{12,4},{16,24},{20,28},{24,16},{28,20},{1,9},{5... | collective-permute-start | bytes 2457608 | tf_op jit(solution)/shard_map/ppermute | solution.py:58
  578.5 45.4 %collective-permute-start.24 = (bf16[2,160,1280]{2,1,0:T(8,128)(2,1)S(1)}, bf16[2,160,1280]{2,1,0:T(8,128)(2,1)S(1)}, u32[]{:S(2)}, u32[]{:S(2)}) collective-permute-start(bf16[2,160,1280]{2,1,0:T(8,128)(2,1)S(1)} %dynamic-slice_bitcast_fusion.5), channel_id=1, source_target_pairs={{0,8},{4,12},{8,0},{12,4},{16,24},{20,28},{24,16},{28,20},{1,9},{5... | collective-permute-start | bytes 2457608 | tf_op jit(solution)/shard_map/ppermute | solution.py:58
  581.6 27.3 %collective-permute-start.34 = (bf16[1,160,1280]{2,1,0:T(8,128)(2,1)S(1)}, bf16[1,160,1280]{2,1,0:T(8,128)(2,1)S(1)}, u32[]{:S(2)}, u32[]{:S(2)}) collective-permute-start(bf16[1,160,1280]{2,1,0:T(8,128)(2,1)S(1)} %constant_dynamic-slice_fusion.3), channel_id=1, source_target_pairs={{0,16},{4,20},{8,24},{12,28},{16,0},{20,4},{24,8},{28,12},{1,17},{... | collective-permute-start | bytes 1228808 | tf_op jit(solution)/shard_map/ppermute | solution.py:58
  582.1 41.6 %collective-permute-start.30 = (bf16[1,160,1280]{2,1,0:T(8,128)(2,1)S(1)}, bf16[1,160,1280]{2,1,0:T(8,128)(2,1)S(1)}, u32[]{:S(2)}, u32[]{:S(2)}) collective-permute-start(bf16[1,160,1280]{2,1,0:T(8,128)(2,1)S(1)} %constant_dynamic-slice_fusion.2), channel_id=1, source_target_pairs={{0,16},{4,20},{8,24},{12,28},{16,0},{20,4},{24,8},{28,12},{1,17},{... | collective-permute-start | bytes 1228808 | tf_op jit(solution)/shard_map/ppermute | solution.py:58
  624.1 11.5 %collective-permute-start.25 = (bf16[1,160,1280]{2,1,0:T(8,128)(2,1)S(1)}, bf16[1,160,1280]{2,1,0:T(8,128)(2,1)S(1)}, u32[]{:S(2)}, u32[]{:S(2)}) collective-permute-start(bf16[1,160,1280]{2,1,0:T(8,128)(2,1)S(1)} %constant_dynamic-slice_fusion.1), channel_id=1, source_target_pairs={{0,16},{4,20},{8,24},{12,28},{16,0},{20,4},{24,8},{28,12},{1,17},{... | collective-permute-start | bytes 1228808 | tf_op jit(solution)/shard_map/ppermute | solution.py:58
  (64 other events, 377.3 us)

commit v2 on v1

v2 whole, which is shorter than its diff:
```python
import jax
import jax.numpy as jnp
from jax import lax
from jax.experimental import pallas as pl
from jax.experimental.pallas import tpu as pltpu
from jax.sharding import PartitionSpec as P

HEAD_DIM = 80
norm_eps = 1e-05
VEC_ROWS = 8
TILE = 256
FIRST_TILES = 3


def low(values):
    return values.astype(jnp.bfloat16)


def wide(values):
    return values.astype(jnp.float32)


def mm(left, right):
    return jnp.dot(left, right, preferred_element_type=jnp.float32)


def mm_left(left, right):
    return lax.dot_general(left, right, (((0,), (0,)), ((), ())), preferred_element_type=jnp.float32)


def mm_right(left, right):
    return lax.dot_general(left, right, (((1,), (1,)), ((), ())), preferred_element_type=jnp.float32)


def norm_parts(values):
    center = values - jnp.mean(values, axis=-1, keepdims=True)
    spread = jnp.mean(center * center, axis=-1, keepdims=True)
    inverse = lax.rsqrt(spread + norm_eps)
    return center * inverse, inverse


def norm_back(grad, xhat, inverse, gain):
    scaled = grad * gain
    first = jnp.mean(scaled, axis=-1, keepdims=True)
    second = jnp.mean(scaled * xhat, axis=-1, keepdims=True)
    return (scaled - first - xhat * second) * inverse


def gelu_pair(pre):
    half = 0.5 * (1.0 + lax.erf(pre * (0.5 ** 0.5)))
    slope = half + pre * jnp.exp(-0.5 * pre * pre) * 0.3989422804014327
    return pre * half, slope


def tensor_swap(values, mask):
    size = lax.axis_size("tensor")
    return lax.ppermute(values, "tensor", [(i, i ^ mask) for i in range(size)])


def data_swap(values, mask):
    size = lax.axis_size("dp")
    return lax.ppermute(values, "dp", [(i, i ^ mask) for i in range(size)])


def masks_of(size):
    masks = []
    while size > 1:
        size //= 2
        masks.append(size)
    return masks


def pin(values, *others):
    return lax.optimization_barrier((values, others))[0]


def after(values, *others):
    return pin(values, *others) if others else values


class Gather:
    def __init__(self, halves):
        self.masks = masks_of(lax.axis_size("dp"))
        self.held = [item[None] for item in halves]
        self.fresh = [None, None]
        self.order = [[0], [0]]
        self.step = 0

    def mask(self, side):
        count = len(self.masks)
        if side == 1 and self.step >= count - 2:
            return self.masks[2 * count - 3 - self.step]
        return self.masks[self.step]

    def advance(self, *others):
        for side in range(2):
            if self.fresh[side] is not None:
                self.held[side] = jnp.concatenate([self.held[side], self.fresh[side]], axis=0)
            mask = self.mask(side)
            self.fresh[side] = data_swap(after(self.held[side], *others), mask)
            self.order[side] = self.order[side] + [item ^ mask for item in self.order[side]]
        self.step += 1
        return tuple(self.fresh)

    def early(self, *others):
        got = ()
        while self.step < len(self.masks) - 2:
            got = self.advance(*others)
        return got


def vmem(count):
    return [pl.BlockSpec(memory_space=pltpu.VMEM)] * count


def settle(*items):
    gathers = [item for item in items if isinstance(item, Gather)]
    others = [item for item in items if not isinstance(item, Gather)]
    arrays = [(item.held, item.fresh) for item in gathers]
    arrays, others = lax.optimization_barrier((arrays, others))
    for item, (held, fresh) in zip(gathers, arrays):
        item.held, item.fresh = list(held), list(fresh)
    return others


def place_body(gathered, depth, extra, joined, me_ref, *refs):
    pieces, outs, sems = refs[:4], refs[4:-1], refs[-1]
    me = me_ref[0]
    copies = []
    for side in range(2):
        held, fresh = pieces[2 * side : 2 * side + 2]
        columns = held.shape[2]
        for position, item in enumerate(gathered.order[side]):
            count = held.shape[0]
            piece, row = (held, position) if position < count else (fresh, position - count)
            if joined:
                target = outs[0].at[me ^ item, pl.ds(0, depth), pl.ds(side * columns, columns)]
            else:
                target = outs[side].at[me ^ item]
            source = piece.at[row, pl.ds(0, depth)] if extra else piece.at[row]
            copies.append(pltpu.make_async_copy(source, target, sems.at[len(copies)]))
            if extra and side == 0:
                source = piece.at[row, pl.ds(depth, extra)]
                copies.append(pltpu.make_async_copy(source, outs[-1].at[me ^ item], sems.at[len(copies)]))
    for item in copies:
        item.start()
    for item in copies:
        item.wait()


def place_blocks(gathered, depth, extra=0, joined=False):
    size = lax.axis_size("dp")
    pieces = [gathered.held[0], gathered.fresh[0], gathered.held[1], gathered.fresh[1]]
    columns = pieces[0].shape[2]
    if extra and depth % 8:
        whole = place_blocks(gathered, depth + extra, 0, joined)
        return [item[:, :depth] for item in whole] + [whole[0][:, depth:, :columns]]
    me = lax.axis_index("dp").reshape(1)
    main = jax.ShapeDtypeStruct((size, depth, (2 if joined else 1) * columns), jnp.bfloat16)
    shapes = [main] if joined else [main, main]
    if extra:
        shapes.append(jax.ShapeDtypeStruct((size, extra, columns), jnp.bfloat16))
    return pl.pallas_call(
        lambda *refs: place_body(gathered, depth, extra, joined, *refs),
        in_specs=[pl.BlockSpec(memory_space=pltpu.SMEM)] + [pl.BlockSpec(memory_space=pl.ANY)] * 4,
        out_specs=vmem(len(shapes)),
        out_shape=shapes,
        compiler_params=pltpu.CompilerParams(vmem_limit_bytes=16 << 20),
        scratch_shapes=[pltpu.SemaphoreType.DMA((3 * size if extra else 2 * size,))],
        cost_estimate=pl.CostEstimate(flops=1024, bytes_accessed=1024, transcendentals=0),
        name="place",
    )(me, *pieces)


class Scatter:
    def __init__(self, own, other):
        size = lax.axis_size("dp")
        self.bits = size.bit_length() - 1
        shape = (2,) * self.bits + (own[0].shape[0] // size, own[0].shape[1])
        self.terms = [[own[side].reshape(shape), other[side].reshape(shape)] for side in range(2)]
        self.axes = [list(range(self.bits)) for side in range(2)]
        masks = masks_of(size)[::-1]
        self.masks = [masks, [masks[1], masks[0]] + masks[2:]]
        self.step = 0

    def part(self, side, index):
        total = None
        for term in self.terms[side]:
            item = wide(lax.dynamic_index_in_dim(term, index, axis=self.where, keepdims=False))
            total = item if total is None else total + item
        return total

    def advance(self, *others):
        me = lax.axis_index("dp")
        sends, kept, masks = [], [], []
        for side in range(2):
            mask = self.masks[side][self.step]
            number = self.bits - mask.bit_length()
            self.where = self.axes[side].index(number)
            bit = (me // mask) % 2
            sends.append(low(self.part(side, 1 - bit)))
            kept.append(self.part(side, bit))
            self.axes[side].remove(number)
            masks.append(mask)
        sends = after(sends, *others)
        self.terms = [[keep, data_swap(send, mask)] for keep, send, mask in zip(kept, sends, masks)]
        self.step += 1

    def finish(self):
        return [wide(item[0]) + wide(item[1]) for item in self.terms]

    def rest(self):
        while self.step < self.bits:
            self.advance()


def settle_scatters(scatters, *others):
    gots = [[item.terms[side][1] for side in range(2)] for item in scatters]
    gots, others = lax.optimization_barrier((gots, others))
    for item, got in zip(scatters, gots):
        for side in range(2):
            item.terms[side][1] = got[side]
    return others


def ff_body(first, tiles, half, *refs):
    n2, cot, n2t, cott, own_up, own_down, sib_up, sib_down, own_b, sib_b = refs[:10]
    refs = refs[10:]
    if not first:
        prev_b, prev_g = refs[:2]
        refs = refs[2:]
    if first:
        acc_b, acc_g = refs[:2]
        own_gu, own_gd, sib_gu, sib_gd, b_own, b_sib = refs[2:]
    else:
        out_keep, out_send, grad_keep, grad_one, grad_two, *refs = refs
        own_gu, own_gd, sib_gu, sib_gd, b_own, b_sib, acc_b, acc_g = refs
    side, tile = pl.program_id(0), pl.program_id(1)

    @pl.when((side == 0) & (tile == 0))
    def _():
        if first:
            acc_b[...] = jnp.zeros_like(acc_b)
            acc_g[...] = jnp.zeros_like(acc_g)
        else:
            acc_b[...] = prev_b[...]
            acc_g[...] = prev_g[...]

    def step(up_ref, down_ref, bias, up_grad, down_grad, bias_sum):
        up, down = up_ref[...], down_ref[...]
        pre = mm(n2[...], up) + wide(bias[...])
        act, slope = gelu_pair(pre)
        hidden = low(act)
        grad_pre = low(mm(cot[...], down) * slope)
        acc_b[...] += mm_right(hidden, down)
        acc_g[...] += mm_right(grad_pre, up)
        up_grad[...] = low(mm(n2t[...], grad_pre))
        down_grad[...] = low(mm(cott[...], hidden))
        bias_sum[...] = jnp.sum(wide(grad_pre), axis=0, keepdims=True)

    @pl.when(side == 0)
    def _():
        step(sib_up, sib_down, sib_b, sib_gu, sib_gd, b_sib)

    @pl.when(side == 1)
    def _():
        step(own_up, own_down, own_b, own_gu, own_gd, b_own)

    if not first:

        @pl.when((side == 1) & (tile == tiles - 1))
        def _():
            out_keep[...] = acc_b[:half]
            out_send[...] = low(acc_b[half:])
            grad_keep[...] = acc_g[...]
            grad_one[...] = low(acc_g[half:])
            grad_two[...] = low(acc_g[:half])


def prepare_body(columns, *refs):
    vectors, (w_query, w_key, w_value, w_out_t), (first, second) = refs[:6], refs[6:10], refs[10:]
    depth, width = w_query.shape
    joined = jnp.concatenate([w_query[...], w_key[...], w_value[...], w_out_t[...]], axis=1)
    first[:depth] = joined[:, :columns]
    second[:depth] = joined[:, columns:]
    first[depth:] = jnp.zeros_like(first[depth:])
    second[depth:] = jnp.zeros_like(second[depth:])
    for k, vector in enumerate(vectors):
        first[depth + k : depth + k + 1, :depth] = vector[...]


def prepare(vectors, weights):
    depth, width = weights[0].shape
    columns = 2 * width
    vectors = [item.reshape(1, depth) for item in vectors]
    return pl.pallas_call(
        lambda *refs: prepare_body(columns, *refs),
        in_specs=vmem(10),
        out_specs=vmem(2),
        out_shape=[jax.ShapeDtypeStruct((depth + VEC_ROWS, columns), jnp.bfloat16)] * 2,
        cost_estimate=pl.CostEstimate(flops=1024, bytes_accessed=1024, transcendentals=0),
        name="prepare",
    )(*vectors, *weights)


def feed_forward(n2, cot, n2t, cott, own_w, sib_w, own_b, sib_b, tile, previous=None):
    rows, model = n2.shape
    hidden = own_b.shape[1]
    tiles = hidden // tile
    first = previous is None
    half = rows // 2

    def const(shape):
        return pl.BlockSpec(shape, lambda s, i: (0, 0), pipeline_mode=pl.Buffered(1))

    def second(shape):
        return pl.BlockSpec(shape, lambda s, i: (0, jnp.where(s == 1, i, 0)))

    def initial(shape):
        return pl.BlockSpec(shape, lambda s, i: (0, jnp.where(s == 0, i, tiles - 1)))

    in_specs = [const((rows, model))] * 2 + [const((model, rows))] * 2
    in_specs += [second((model, tile))] * 2 + [initial((model, tile))] * 2 + [second((1, tile)), initial((1, tile))]
    operands = [n2, cot, n2t, cott, *own_w, *sib_w, own_b, sib_b]
    full = jax.ShapeDtypeStruct((rows, model), jnp.float32)
    grads = jax.ShapeDtypeStruct((model, hidden), jnp.bfloat16)
    sums = jax.ShapeDtypeStruct((1, hidden), jnp.float32)
    tail_shapes = [grads] * 4 + [sums, sums]
    tail_specs = [second((model, tile))] * 2 + [initial((model, tile))] * 2 + [second((1, tile)), initial((1, tile))]
    scratch = []
    if first:
        shapes = [full, full] + tail_shapes
        specs = [const((rows, model))] * 2 + tail_specs
    else:
        operands += list(previous)
        in_specs += [const((rows, model))] * 2
        shapes = [
            jax.ShapeDtypeStruct((half, model), jnp.float32),
            jax.ShapeDtypeStruct((half, model), jnp.bfloat16),
            full,
            jax.ShapeDtypeStruct((half, model), jnp.bfloat16),
            jax.ShapeDtypeStruct((half, model), jnp.bfloat16),
        ] + tail_shapes
        specs = [const((half, model))] * 2 + [const((rows, model))] + [const((half, model))] * 2 + tail_specs
        scratch = [pltpu.VMEM((rows, model), jnp.float32)] * 2
    return pl.pallas_call(
        lambda *refs: ff_body(first, tiles, half, *refs),
        grid=(2, tiles),
        in_specs=in_specs,
        out_specs=specs,
        out_shape=shapes,
        scratch_shapes=scratch,
        compiler_params=pltpu.CompilerParams(vmem_limit_bytes=56 << 20),
        cost_estimate=pl.CostEstimate(flops=1024, bytes_accessed=1024, transcendentals=0),
        name="feed_forward",
    )(*operands)


def dot_t(left, right):
    return lax.dot_general(left, right, (((0,), (0,)), ((), ())), preferred_element_type=jnp.float32)


def norm_rows(values, gain, shift):
    xhat, inverse = norm_parts(values)
    return low(xhat * gain + shift)


def attn_head(joined, head, width, mask):
    scale = HEAD_DIM ** (-0.5)
    begin = pl.multiple_of(head * HEAD_DIM, 16)
    query = joined[pl.ds(begin, HEAD_DIM), :]
    keys = joined[pl.ds(pl.multiple_of(width + begin, 16), HEAD_DIM), :]
    values = joined[pl.ds(pl.multiple_of(2 * width + begin, 16), HEAD_DIM), :]
    scores = jnp.where(mask[...] > 0.5, dot_t(keys, query) * scale, -1000000000.0)
    return begin, query, keys, values, scores


def attn_forward_body(first, width, *refs):
    if first:
        x, gain, shift, weights, bias, mask, n1, n1t, joined, mixed, totals, part = refs
        n1[...] = norm_rows(wide(x[...]), gain[...], shift[...])
        n1t[...] = n1[...].T
    else:
        n1, previous, weights, bias, mask, joined, mixed, totals, part, send_one, send_two = refs
    joined[...] = low(mm(n1[...], weights[:, : 3 * width]) + bias[...]).T

    def one(head, carry):
        begin, query, keys, values, scores = attn_head(joined, head, width, mask)
        top = jnp.max(scores, axis=0, keepdims=True)
        expo = jnp.exp(scores - top)
        total = jnp.sum(expo, axis=0, keepdims=True)
        probs = low(expo * (1.0 / total))
        mixed[pl.ds(begin, HEAD_DIM), :] = low(mm(values, probs))
        totals[pl.ds(head, 1), :] = top + jnp.log(total)
        return carry

    lax.fori_loop(0, width // HEAD_DIM, one, 0)
    term = mm_right(mixed[...].T, weights[:, 3 * width :])
    if first:
        part[...] = term
    else:
        term = previous[...] + term
        half = term.shape[0] // 2
        part[...] = term
        send_one[...] = low(term[half:])
        send_two[...] = low(term[:half])


def attn_forward(head_in, weights, bias, mask, width, first):
    rows, model = head_in[0].shape
    low_shape = lambda *shape: jax.ShapeDtypeStruct(shape, jnp.bfloat16)
    wide_shape = lambda *shape: jax.ShapeDtypeStruct(shape, jnp.float32)
    shapes = [low_shape(3 * width, rows), low_shape(width, rows), wide_shape(width // HEAD_DIM, rows), wide_shape(rows, model)]
    shapes = [low_shape(rows, model), low_shape(model, rows)] + shapes if first else shapes + [low_shape(rows // 2, model)] * 2
    operands = list(head_in) + [weights, bias, mask]
    return pl.pallas_call(
        lambda *refs: attn_forward_body(first, width, *refs),
        in_specs=vmem(len(operands)),
        out_specs=vmem(len(shapes)),
        out_shape=shapes,
        compiler_params=pltpu.CompilerParams(vmem_limit_bytes=56 << 20),
        cost_estimate=pl.CostEstimate(flops=1024, bytes_accessed=1024, transcendentals=0),
        name="attn_forward",
    )(*operands)


def attn_backward_body(first, width, half, *refs):
    gb, gbt, n1t, weights, joined, mixed, totals, mask = refs[:8]
    refs = refs[8:]
    if first:
        part, grads_one, grads_two, sums, gmt, djoined = refs
    else:
        previous, keep, send, grads_one, grads_two, sums, gmt, djoined = refs
    scale = HEAD_DIM ** (-0.5)
    gmt[...] = low(mm(gb[...], weights[:, 3 * width :])).T

    def one(head, carry):
        begin, query, keys, values, scores = attn_head(joined, head, width, mask)
        probs = jnp.exp(scores - totals[pl.ds(head, 1), :])
        gm = gmt[pl.ds(begin, HEAD_DIM), :]
        grad_probs = dot_t(values, gm)
        delta = jnp.sum(grad_probs * probs, axis=0, keepdims=True)
        grad_scores = low(probs * (grad_probs - delta))
        djoined[pl.ds(begin, HEAD_DIM), :] = low(mm(keys, grad_scores) * scale)
        djoined[pl.ds(pl.multiple_of(width + begin, 16), HEAD_DIM), :] = low(mm_right(query, grad_scores) * scale)
        djoined[pl.ds(pl.multiple_of(2 * width + begin, 16), HEAD_DIM), :] = low(mm_right(gm, low(probs)))
        return carry

    lax.fori_loop(0, width // HEAD_DIM, one, 0)
    grads_one[...] = low(mm_right(n1t[...], djoined[: 2 * width]))
    grads_two[:, :width] = low(mm_right(n1t[...], djoined[2 * width :]))
    grads_two[:, width:] = low(mm_right(gbt[...], mixed[...]))
    ones = jnp.ones((8, gb.shape[0]), jnp.bfloat16)
    sums[...] = mm_right(ones, djoined[...])
    term = mm_right(djoined[...].T, weights[:, : 3 * width])
    if first:
        part[...] = term
    else:
        term = previous[...] + term
        keep[...] = term[:half]
        send[...] = low(term[half:])


def attn_backward(gb, gbt, n1t, weights, saved, mask, width, previous=None):
    rows, model = gb.shape
    first = previous is None
    half = rows // 2
    operands = [gb, gbt, n1t, weights, *saved, mask]
    shapes = [jax.ShapeDtypeStruct((model, 2 * width), jnp.bfloat16)] * 2 + [jax.ShapeDtypeStruct((8, 3 * width), jnp.float32)]
    if first:
        shapes = [jax.ShapeDtypeStruct((rows, model), jnp.float32)] + shapes
    else:
        operands.append(previous)
        shapes = [
            jax.ShapeDtypeStruct((half, model), jnp.float32),
            jax.ShapeDtypeStruct((half, model), jnp.bfloat16),
        ] + shapes
    return pl.pallas_call(
        lambda *refs: attn_backward_body(first, width, half, *refs),
        in_specs=vmem(len(operands)),
        out_specs=vmem(len(shapes)),
        out_shape=shapes,
        scratch_shapes=[pltpu.VMEM((width, rows), jnp.bfloat16), pltpu.VMEM((3 * width, rows), jnp.bfloat16)],
        compiler_params=pltpu.CompilerParams(vmem_limit_bytes=56 << 20),
        cost_estimate=pl.CostEstimate(flops=1024, bytes_accessed=1024, transcendentals=0),
        name="attn_backward",
    )(*operands)


def middle_body(half, x, part, got_first, got_second, bias, gain, shift, inner, n2, n2t):
    for k, got in enumerate((got_first, got_second)):
        part_rows = slice(k * half, (k + 1) * half)
        value = wide(x[part_rows]) + (part[part_rows] + wide(got[...]) + bias[...])
        inner[part_rows] = value
        n2[part_rows] = norm_rows(value, gain[...], shift[...])
    n2t[...] = n2[...].T


def middle(x, part, got_first, got_second, bias, gain, shift):
    rows, model = x.shape
    shapes = [
        jax.ShapeDtypeStruct((rows, model), jnp.float32),
        jax.ShapeDtypeStruct((rows, model), jnp.bfloat16),
        jax.ShapeDtypeStruct((model, rows), jnp.bfloat16),
    ]
    return pl.pallas_call(
        lambda *refs: middle_body(rows // 2, *refs),
        in_specs=vmem(7),
        out_specs=vmem(3),
        out_shape=shapes,
        compiler_params=pltpu.CompilerParams(vmem_limit_bytes=40 << 20),
        cost_estimate=pl.CostEstimate(flops=1024, bytes_accessed=1024, transcendentals=0),
        name="middle",
    )(x, part, got_first, got_second, bias, gain, shift)


def turn_body(half, inner, grad, got_first, got_second, cot, gain, keep, gb, gbt, vectors):
    for k, got in enumerate((got_first, got_second)):
        part_rows = slice(k * half, (k + 1) * half)
        value = grad[part_rows] + wide(got[...])
        xhat, inverse = norm_parts(inner[part_rows])
        top = wide(cot[part_rows])
        total = top + norm_back(value, xhat, inverse, gain[...])
        gb[part_rows] = low(total)
        if k == 0:
            keep[...] = total
            vectors[0:1, :] = jnp.sum(wide(low(total)), axis=0, keepdims=True)
            vectors[1:2, :] = jnp.sum(value * xhat, axis=0, keepdims=True)
            vectors[2:3, :] = jnp.sum(value, axis=0, keepdims=True)
            vectors[3:4, :] = jnp.sum(top, axis=0, keepdims=True)
    gbt[...] = gb[...].T


def turn(inner, grad, got_first, got_second, cot, gain):
    rows, model = inner.shape
    shapes = [
        jax.ShapeDtypeStruct((rows // 2, model), jnp.float32),
        jax.ShapeDtypeStruct((rows, model), jnp.bfloat16),
        jax.ShapeDtypeStruct((model, rows), jnp.bfloat16),
        jax.ShapeDtypeStruct((4, model), jnp.float32),
    ]
    return pl.pallas_call(
        lambda *refs: turn_body(rows // 2, *refs),
        in_specs=vmem(6),
        out_specs=vmem(4),
        out_shape=shapes,
        compiler_params=pltpu.CompilerParams(vmem_limit_bytes=40 << 20),
        cost_estimate=pl.CostEstimate(flops=1024, bytes_accessed=1024, transcendentals=0),
        name="turn",
    )(inner, grad, got_first, got_second, cot, gain)


def pick(pair, index):
    return lax.dynamic_index_in_dim(pair, index, axis=0, keepdims=False)


def order_pair(mine, other, core):
    return jnp.where(core == 0, jnp.stack([mine, other]), jnp.stack([other, mine]))


def shards(
    clips,
    lengths,
    norm1_gain,
    norm1_bias,
    w_query,
    bias_query,
    w_key,
    w_value,
    bias_value,
    w_out,
    bias_out,
    norm2_gain,
    norm2_bias,
    w_up,
    bias_up,
    w_down,
    bias_down,
    cotangent,
):
    rows = clips.shape[1]
    model = clips.shape[2]
    depth, width = w_query.shape
    hidden_width = w_up.shape[1]
    data_size = lax.axis_size("dp")
    place = lax.axis_index("tensor")
    core = place % 2
    masks = masks_of(data_size)

    sent = jnp.concatenate([pick(clips, 1 - core), pick(cotangent, 1 - core)], axis=0)
    vectors = (norm1_gain, norm1_bias, bias_out, norm2_gain, norm2_bias, bias_down)
    attn = Gather(prepare(vectors, (w_query, w_key, w_value, w_out.T)))
    got = tensor_swap(sent, 1)
    half_rows = jnp.concatenate([pick(clips, core), got[:rows], pick(cotangent, core), got[rows:]], axis=0)
    other_half = tensor_swap(half_rows, 2)
    local_bias = jnp.concatenate([bias_up, bias_query, bias_value])
    sib_bias = tensor_swap(local_bias.reshape(1, -1), 1)[0]

    cut = FIRST_TILES * TILE
    down_t = w_down.T
    ff_one = Gather([w_up[:, :cut], down_t[:, :cut]])
    ff_two = Gather([w_up[:, cut:], down_t[:, cut:]])
    attn.early()
    other_half, sib_bias = settle(attn, ff_one, ff_two, other_half, sib_bias)
    attn.advance()
    ff_one.early()
    low_rows = jnp.concatenate([half_rows[: 2 * rows], other_half[: 2 * rows]], axis=0)
    cot = jnp.concatenate([half_rows[2 * rows :], other_half[2 * rows :]], axis=0)
    cott = cot.T
    low_rows, cot, cott = settle(attn, ff_one, low_rows, cot, cott)
    attn.advance()
    ff_one.advance()
    ff_two.early()
    length = pick(lengths, core)
    block = place ^ lax.iota(jnp.int32, 4)
    position = (block[:, None] * rows + lax.iota(jnp.int32, rows)[None, :]).reshape(-1)
    mask = (position < length).astype(jnp.float32).reshape(-1, 1)
    biases = (local_bias.reshape(1, -1), sib_bias.reshape(1, -1))
    joined_biases = []
    for item in biases:
        item = wide(item[:, hidden_width:])
        joined_biases.append(jnp.concatenate([item[:, :width], jnp.zeros((1, width), jnp.float32), item[:, width:]], axis=1))
    mask, joined_biases = settle(attn, ff_one, ff_two, mask, joined_biases)
    ff_one.advance()
    ff_two.advance()

    attn_all, vector_all = place_blocks(attn, depth, VEC_ROWS, True)
    attn_own = attn_all.reshape(model, model)
    attn_sib = tensor_swap(attn_own, 1)
    attn_w = (attn_own, attn_sib)
    vectors_full = wide(vector_all[:, :6, :depth].transpose(1, 0, 2).reshape(6, model))
    gain_one, shift_one, out_bias, gain_two, shift_two, down_bias = [vectors_full[k : k + 1] for k in range(6)]
    outs = attn_forward((low_rows, gain_one, shift_one), attn_own, joined_biases[0], mask, width, True)
    normed_one, n1t = outs[:2]
    saved = [outs[2:5]]
    outs = attn_forward((normed_one, outs[5]), attn_sib, joined_biases[1], mask, width, False)
    saved.append(outs[:3])
    part_keep, *part_send = outs[3:]

    def exchange(send):
        return tensor_swap(send[0], 2), tensor_swap(send[1], 2)

    (part_send,) = settle(ff_one, ff_two, part_send)
    ff_two.advance()
    first, second = exchange(part_send)

    def ff_weights(gathered):
        own_w = [item.reshape(model, -1) for item in place_blocks(gathered, depth)]
        return own_w, [tensor_swap(item, 1) for item in own_w]

    one_own, one_sib = ff_weights(ff_one)
    first, second, one_sib = settle(ff_two, first, second, one_sib)
    two_own, two_sib = ff_weights(ff_two)
    inner, normed_two, n2t = middle(low_rows, part_keep, first, second, out_bias, gain_two, shift_two)
    bias_rows = [[item[:, :cut], item[:, cut:hidden_width]] for item in biases]
    outs = feed_forward(normed_two, cot, n2t, cott, one_own, one_sib, bias_rows[0][0], bias_rows[1][0], TILE)
    one_sums = outs[6:]
    one_grads, one_sent = outs[2:4], [tensor_swap(item, 1) for item in outs[4:6]]
    outs = feed_forward(normed_two, cot, n2t, cott, two_own, two_sib, bias_rows[0][1], bias_rows[1][1], TILE, outs[:2])
    out_keep, out_send, grad_keep, *grad_send = outs[:5]
    two_sums = outs[9:]
    two_grads, two_sent = outs[5:7], [tensor_swap(item, 1) for item in outs[7:9]]

    first, second = exchange(grad_send)
    scatter_one, scatter_two = Scatter(one_grads, one_sent), Scatter(two_grads, two_sent)
    scatter_one.advance()
    first, second, out_send, two_sent = settle_scatters([scatter_one], first, second, out_send, two_sent)
    out_got = tensor_swap(out_send, 2)
    scatter_one.advance()
    scatter_two.advance()
    inner_keep, grad_branch, gbt, vectors_two = turn(inner, grad_keep, first, second, cot, gain_two)
    part, *other_grads, other_sums = attn_backward(grad_branch, gbt, n1t, attn_w[1], saved[1], mask, width)
    part, out_got, other_grads = settle_scatters([scatter_one, scatter_two], part, out_got, other_grads)
    scatter_one.advance()
    scatter_two.advance()
    attn_sent = [tensor_swap(item, 1) for item in other_grads]
    one_keep, one_send, *own_grads, own_sums = attn_backward(grad_branch, gbt, n1t, attn_w[0], saved[0], mask, width, part)
    own_grads, one_send, attn_sent, out_got = settle_scatters([scatter_one, scatter_two], own_grads, one_send, attn_sent, out_got)
    scatter_attn = Scatter(own_grads, attn_sent)
    scatter_one.rest()
    scatter_two.advance()
    scatter_attn.advance()
    one_got = tensor_swap(one_send, 2)
    one_got, out_got = settle_scatters([scatter_two, scatter_attn], one_got, out_got)
    scatter_two.rest()
    scatter_attn.advance()

    out_half = inner[: 2 * rows] + (out_keep + wide(out_got) + down_bias)
    out_low = low(out_half)
    output = order_pair(out_low[:rows], tensor_swap(out_low[rows:], 1), core)
    xhat_one, inverse_one = norm_parts(wide(low_rows[: 2 * rows]))
    grad_normed_one = one_keep + wide(one_got)
    v_gain_one = jnp.sum(grad_normed_one * xhat_one, axis=0, keepdims=True)
    v_shift_one = jnp.sum(grad_normed_one, axis=0, keepdims=True)
    clip_half = inner_keep + norm_back(grad_normed_one, xhat_one, inverse_one, gain_one)
    clip_grad = order_pair(clip_half[:rows], tensor_swap(clip_half[rows:], 1), core)

    small = jnp.concatenate([v_gain_one, v_shift_one, vectors_two], axis=0)

    def bias_pair(up_sums, sums):
        first_row = jnp.pad(jnp.concatenate(up_sums, axis=1), ((0, 0), (0, model - hidden_width)))
        second_row = jnp.concatenate([sums[:1, :width], sums[:1, 2 * width :], jnp.zeros((1, model - 2 * width), jnp.float32)], axis=1)
        return jnp.concatenate([first_row, second_row], axis=0)

    from_sib = tensor_swap(jnp.concatenate([small, bias_pair((one_sums[1], two_sums[1]), other_sums)], axis=0), 1)
    small = small + from_sib[:6]
    small = small + tensor_swap(small, 2)
    small = jnp.concatenate([small, bias_pair((one_sums[0], two_sums[0]), own_sums) + from_sib[6:]], axis=0)
    for mask_bit in masks[::-1]:
        small = small + data_swap(small, mask_bit)
    vector_own = lax.dynamic_slice_in_dim(small[:6], lax.axis_index("dp") * depth, depth, axis=1)

    scatter_attn.rest()
    one_up, one_down = scatter_one.finish()
    two_up, two_down = scatter_two.finish()
    attn_one, attn_two = scatter_attn.finish()
    return (
        output,
        clip_grad,
        vector_own[0],
        vector_own[1],
        attn_one[:, :width],
        small[7, :width],
        attn_one[:, width:],
        attn_two[:, :width],
        small[7, width : 2 * width],
        attn_two[:, width:].T,
        vector_own[2],
        vector_own[3],
        vector_own[4],
        jnp.concatenate([one_up, two_up], axis=1),
        small[6, :hidden_width],
        jnp.concatenate([one_down, two_down], axis=1).T,
        vector_own[5],
    )


def solution(mesh):
    rows_spec = P("dp", "tensor", None)
    data, tensor = P("dp"), P("tensor")
    wide_spec, tall_spec = P("dp", "tensor"), P("tensor", "dp")
    placed = (
        rows_spec,
        data,
        data,
        data,
        wide_spec,
        tensor,
        wide_spec,
        wide_spec,
        tensor,
        tall_spec,
        data,
        data,
        data,
        wide_spec,
        tensor,
        tall_spec,
        data,
        rows_spec,
    )
    outs = (
        rows_spec,
        rows_spec,
        data,
        data,
        wide_spec,
        tensor,
        wide_spec,
        wide_spec,
        tensor,
        tall_spec,
        data,
        data,
        data,
        wide_spec,
        tensor,
        tall_spec,
        data,
    )
    return jax.shard_map(shards, mesh=mesh, in_specs=placed, out_specs=outs, check_vma=False)
```

time: 644 us -> 454 us (0.70)
  waiting for transfers between devices: 295 us -> 164 us
  Pallas kernels: 0 us -> 108 us
  matrix products: 98.8 us -> 0 us
  blocking collectives: 59.2 us -> 0 us
  starting transfers between devices: 39.5 us -> 62.3 us
  between operations: 18.1 us -> 1.93 us
  other arithmetic: 62.9 us -> 54.2 us
    ppermute x18 -> x39, waiting for transfers between devices: 242 us -> 124 us  [data_swap(): return lax.ppermute(values, 'dp', [(i, i ^ mask) for i in range(size)])]
    pallas_call x0 -> x12, Pallas kernels: none -> 108 us  [the longest x2 42.1 us: feed_forward(): pl.pallas_call(lambda *refs: ff_body(first, tiles, half, *refs), grid=(2,...]
    dot_general x48 -> x0, matrix products: 98.8 us -> none  [the longest x12 32.6 us: mm_right(): lax.dot_general(left, right, (((1,), (1,)), ((), ())), preferred_element_...]
    psum x2 -> x0, blocking collectives: 59.2 us -> none  [the longest x1 37.4 us: shards(): vector_total = lax.psum(vector_total, ('dp', 'tensor'))]
    add x6 -> x22, other arithmetic: 3.03 us -> 22.3 us  [the longest x9 17.7 us: part(): total = item if total is None else total + item]
    ppermute x18 -> x39, starting transfers between devices: 30.4 us -> 47.8 us  [data_swap(): return lax.ppermute(values, 'dp', [(i, i ^ mask) for i in range(size)])]
    convert_element_type x3 -> x0, local copies, waits for them, and re-layouts: 15.3 us -> none  [low(): return values.astype(jnp.bfloat16)]
    ppermute x17 -> x24, waiting for transfers between devices: 52.7 us -> 40.3 us  [tensor_swap(): return lax.ppermute(values, 'tensor', [(i, i ^ mask) for i in range(size)])]
  transfers between devices with their start and end apart: 35 -> 63, of which waited for: 18 -> 24; matrix products, arithmetic and copies ran while one was open for 33% -> 19% of each run, Pallas kernels for 0% -> 22%
where the time goes in v2:
time: 454 us; the launch traced here: 450 us
  waiting for transfers between devices  164 us (36%)
  Pallas kernels  108 us (24%)
  starting transfers between devices  62.3 us (14%)
  local copies, waits for them, and re-layouts  58.9 us (13%)
  other arithmetic  54.2 us (12%)
    ppermute x39, waiting for transfers between devices, data_swap(): return lax.ppermute(values, 'dp', [(i, i ^ mask) for i in range(size)])  124 us
    ppermute x39, starting transfers between devices, data_swap(): return lax.ppermute(values, 'dp', [(i, i ^ mask) for i in range(size)])  47.8 us
    pallas_call x2, Pallas kernels, feed_forward(): pl.pallas_call(lambda *refs: ff_body(first, tiles, half, *refs), grid=(2,...  42.1 us
    ppermute x24, waiting for transfers between devices, tensor_swap(): return lax.ppermute(values, 'tensor', [(i, i ^ mask) for i in range(size)])  40.3 us
    pallas_call x2, Pallas kernels, attn_backward(): pl.pallas_call(lambda *refs: attn_backward_body(first, width, half, *refs...  31.7 us
    unnamed x186, local copies, waits for them, and re-layouts  24.8 us
    pallas_call x2, Pallas kernels, attn_forward(): pl.pallas_call(lambda *refs: attn_forward_body(first, width, *refs), in_s...  20.8 us
    convert_element_type x16, other arithmetic, low(): return values.astype(jnp.bfloat16)  17.8 us
  transfers between devices with their start and end apart: 63, of which 24 were waited for; matrix products, arithmetic and copies ran while one was open for 19% of the time, Pallas kernels for 22%

profile of v2, /device:TPU:0, one launch (start us, length us, event | category | flops | bytes accessed | tf_op | source)
XLA Modules:
  0.0 449.8 jit_solution(12279708260435711596)
XLA Ops:
  5.7 2.9 collective-permute-start.3
  11.9 2.0 prepare.1
  14.0 2.6 collective-permute-start
  20.8 11.8 %collective-permute-done = bf16[1,168,640]{2,1,0:T(8,128)(2,1)} collective-permute-done((bf16[1,168,640]{2,1,0:T(8,128)(2,1)}, bf16[1,168,640]{2,1,0:T(8,128)(2,1)}, u32[]{:S(2)}, u32[]{:S(2)}) %collective-permute-start) | collective-permute-done | bytes 215072 | tf_op jit(solution)/shard_map/ppermute | solution.py:62
  32.6 3.5 collective-permute-done.1
  40.7 1.9 collective-permute-start.5
  45.1 2.6 collective-permute-start.7
  49.7 2.6 collective-permute-start.13
  53.5 15.5 %collective-permute-done.7 = bf16[1,160,768]{2,1,0:T(8,128)(2,1)S(1)} collective-permute-done((bf16[1,160,768]{2,1,0:T(8,128)(2,1)S(1)}, bf16[1,160,768]{2,1,0:T(8,128)(2,1)S(1)}, u32[]{:S(2)}, u32[]{:S(2)}) %collective-permute-start.7) | collective-permute-done | bytes 245792 | tf_op jit(solution)/shard_map/ppermute | solution.py:62
  68.9 4.9 %collective-permute-done.8 = bf16[1,160,768]{2,1,0:T(8,128)(2,1)S(1)} collective-permute-done((bf16[1,160,768]{2,1,0:T(8,128)(2,1)S(1)}, bf16[1,160,768]{2,1,0:T(8,128)(2,1)S(1)}, u32[]{:S(2)}, u32[]{:S(2)}) %collective-permute-start.8) | collective-permute-done | bytes 245792 | tf_op jit(solution)/shard_map/ppermute | solution.py:62
  74.7 2.1 collective-permute-start.11
  80.1 23.2 %collective-permute-done.14 = bf16[1,160,512]{2,1,0:T(8,128)(2,1)S(1)} collective-permute-done((bf16[1,160,512]{2,1,0:T(8,128)(2,1)S(1)}, bf16[1,160,512]{2,1,0:T(8,128)(2,1)S(1)}, u32[]{:S(2)}, u32[]{:S(2)}) %collective-permute-start.14) | collective-permute-done | bytes 163872 | tf_op jit(solution)/shard_map/ppermute | solution.py:62
  103.3 4.6 %collective-permute-done.11 = bf16[2,160,768]{2,1,0:T(8,128)(2,1)S(1)} collective-permute-done((bf16[2,160,768]{2,1,0:T(8,128)(2,1)S(1)}, bf16[2,160,768]{2,1,0:T(8,128)(2,1)S(1)}, u32[]{:S(2)}, u32[]{:S(2)}) %collective-permute-start.11) | collective-permute-done | bytes 491552 | tf_op jit(solution)/shard_map/ppermute | solution.py:62
  114.2 2.0 collective-permute-start.18
  121.5 10.2 %attn_forward.2 = (bf16[512,1280]{1,0:T(8,128)(2,1)}, bf16[1280,512]{1,0:T(8,128)(2,1)}, bf16[960,512]{1,0:T(8,128)(2,1)}, bf16[320,512]{1,0:T(8,128)(2,1)}, f32[4,512]{1,0:T(4,128)}, /*index=5*/f32[512,1280]{1,0:T(8,128)}) custom-call(bf16[512,1280]{1,0:T(8,128)(2,1)} %pad_maximum_fusion.2.refs_0_, f32[1,1280]{1,0:T(1,128)} %slice.189.refs_1_, ...), custom_call_target="tpu_custom_call" | custom-call | flops 1024 | bytes 1024 | tf_op jit(solution)/shard_map/attn_forward/pallas_call | solution.py:416
  131.7 10.6 %attn_forward.3 = (bf16[960,512]{1,0:T(8,128)(2,1)}, bf16[320,512]{1,0:T(8,128)(2,1)}, f32[4,512]{1,0:T(4,128)}, f32[512,1280]{1,0:T(8,128)}, bf16[256,1280]{1,0:T(8,128)(2,1)}, /*index=5*/bf16[256,1280]{1,0:T(8,128)(2,1)}) custom-call(bf16[512,1280]{1,0:T(8,128)(2,1)} %get-tuple-element.184.refs_0_, f32[512,1280]{1,0:T(8,128)} %get-tuple-element.185.refs_1_, ...), custom_call_target="tpu_custom_call" | custom-call | flops 1024 | bytes 1024 | tf_op jit(solution)/shard_map/attn_forward/pallas_call | solution.py:416
  144.0 2.3 place.4
  146.9 2.1 constant_dynamic-update-slice_fusion.21
  155.5 10.3 %collective-permute-done.20.refs_2_ = bf16[4,160,512]{2,1,0:T(8,128)(2,1)S(1)} collective-permute-done((bf16[4,160,512]{2,1,0:T(8,128)(2,1)S(1)}, bf16[4,160,512]{2,1,0:T(8,128)(2,1)S(1)}, u32[]{:S(2)}, u32[]{:S(2)}) %collective-permute-start.20) | collective-permute-done | bytes 655392 | tf_op jit(solution)/shard_map/ppermute | solution.py:62
  169.1 2.5 collective-permute-done.22.refs_2_
  172.5 11.0 %collective-permute-done.23.refs_3_ = bf16[256,1280]{1,0:T(8,128)(2,1)S(1)} collective-permute-done((bf16[256,1280]{1,0:T(8,128)(2,1)S(1)}, bf16[256,1280]{1,0:T(8,128)(2,1)S(1)}, u32[]{:S(2)}, u32[]{:S(2)}) %collective-permute-start.23) | collective-permute-done | bytes 655392 | tf_op jit(solution)/shard_map/ppermute | solution.py:57
  184.7 4.6 %place.5 = (bf16[8,160,512]{2,1,0:T(8,128)(2,1)S(1)}, bf16[8,160,512]{2,1,0:T(8,128)(2,1)}) custom-call(s32[1]{0:T(128)} %bitcast.13.refs_0_, bf16[4,160,512]{2,1,0:T(8,128)(2,1)S(1)} %constant_dynamic-update-slice_fusion.20.refs_1_, bf16[4,160,512]{2,1,0:T(8,128)(2,1)S(1)} %collective-permute-done.20.refs_2_, ...), custom_call_target="tpu_custom_call" | custom-call | flops 1024 | bytes 1024 | tf_op jit(solution)/shard_map/place/pallas_call | solution.py:163
  191.1 2.6 copy.52.refs_3_
  201.8 22.4 %feed_forward.2 = (f32[512,1280]{1,0:T(8,128)}, f32[512,1280]{1,0:T(8,128)}, bf16[1280,768]{1,0:T(8,128)(2,1)}, bf16[1280,768]{1,0:T(8,128)(2,1)}, bf16[1280,768...) custom-call(bf16[512,1280]{1,0:T(8,128)(2,1)} %copy-done.6, ...), custom_call_target="tpu_custom_call" | custom-call | flops 1024 | bytes 1024 | tf_op jit(solution)/shard_map/feed_forward/pallas_call | solution.py:346
  225.9 19.7 %feed_forward.3 = (f32[256,1280]{1,0:T(8,128)}, bf16[256,1280]{1,0:T(8,128)(2,1)}, f32[512,1280]{1,0:T(8,128)}, bf16[256,1280]{1,0:T(8,128)(2,1)}, bf16[256,1280...) custom-call(bf16[512,1280]{1,0:T(8,128)(2,1)} %copy-done.6, ...), custom_call_target="tpu_custom_call" | custom-call | flops 1024 | bytes 1024 | tf_op jit(solution)/shard_map/feed_forward/pallas_call | solution.py:346
  246.2 2.6 fusion.11
  249.3 2.5 fusion.12
  263.3 7.9 %collective-permute-done.33.refs_2_ = bf16[256,1280]{1,0:T(8,128)(2,1)S(1)} collective-permute-done((bf16[256,1280]{1,0:T(8,128)(2,1)}, bf16[256,1280]{1,0:T(8,128)(2,1)S(1)}, u32[]{:S(2)}, u32[]{:S(2)}) %collective-permute-start.33) | collective-permute-done | bytes 655392 | tf_op jit(solution)/shard_map/ppermute | solution.py:57
  271.7 12.0 %collective-permute-done.34.refs_3_ = bf16[256,1280]{1,0:T(8,128)(2,1)S(1)} collective-permute-done((bf16[256,1280]{1,0:T(8,128)(2,1)S(1)}, bf16[256,1280]{1,0:T(8,128)(2,1)S(1)}, u32[]{:S(2)}, u32[]{:S(2)}) %collective-permute-start.34) | collective-permute-done | bytes 655392 | tf_op jit(solution)/shard_map/ppermute | solution.py:57
  283.7 2.6 bitcast_add_fusion.1
  288.5 2.5 bitcast_add_fusion
  293.0 2.3 turn.1
  297.5 15.5 %attn_backward.2 = (f32[512,1280]{1,0:T(8,128)}, bf16[1280,640]{1,0:T(8,128)(2,1)}, bf16[1280,640]{1,0:T(8,128)(2,1)}, f32[8,960]{1,0:T(8,128)}) custom-call(bf16[512,1280]{1,0:T(8,128)(2,1)} %copy-done.8, bf16[1280,512]{1,0:T(8,128)(2,1)} %copy-done.9, bf16[1280,512]{1,0:T(8,128)(2,1)} %get-tuple-element.246.refs_2_, ...), custom_call_target="tpu_custom_call" | custom-call | flops 1024 | bytes 1024 | tf_op jit(solution)/shard_map/attn_backward/pallas_call | solution.py:478
  322.0 2.6 collective-permute-start.41
  329.3 13.0 %collective-permute-done.41 = bf16[160,768]{1,0:T(8,128)(2,1)S(1)} collective-permute-done((bf16[160,768]{1,0:T(8,128)(2,1)S(1)}, bf16[160,768]{1,0:T(8,128)(2,1)S(1)}, u32[]{:S(2)}, u32[]{:S(2)}) %collective-permute-start.41) | collective-permute-done | bytes 245792 | tf_op jit(solution)/shard_map/ppermute | solution.py:62
  345.8 16.2 %attn_backward.3 = (f32[256,1280]{1,0:T(8,128)}, bf16[256,1280]{1,0:T(8,128)(2,1)}, bf16[1280,640]{1,0:T(8,128)(2,1)}, bf16[1280,640]{1,0:T(8,128)(2,1)}, f32[8,960]{1,0:T(8,128)}) custom-call(bf16[512,1280]{1,0:T(8,128)(2,1)} %copy-done.8, bf16[1280,512]{1,0:T(8,128)(2,1)} %copy-done.9, bf16[1280,512]{1,0:T(8,128)(2,1)} %get-tuple-element.246.refs_2_, ...), custom_call_target="tpu_custom_call" | custom-call | flops 1024 | bytes 1024 | tf_op jit(solution)/shard_map/attn_backward/pallas_call | solution.py:478
  370.4 3.0 collective-permute-start.50
  377.1 2.6 convert_add_fusion.3
  379.7 2.6 convert_add_fusion.2
  382.3 9.6 %collective-permute-done.48 = bf16[160,512]{1,0:T(8,128)(2,1)S(1)} collective-permute-done((bf16[160,512]{1,0:T(8,128)(2,1)S(1)}, bf16[160,512]{1,0:T(8,128)(2,1)S(1)}, u32[]{:S(2)}, u32[]{:S(2)}) %collective-permute-start.48) | collective-permute-done | bytes 163872 | tf_op jit(solution)/shard_map/ppermute | solution.py:62
  391.9 3.1 collective-permute-done.50
  406.1 3.5 collective-permute-done.55
  411.9 4.2 collective-permute-done.56
  422.8 2.4 collective-permute-done.58
  428.8 2.0 maximum_select_fusion.1
  432.3 9.5 %collective-permute-done.60 = bf16[160,640]{1,0:T(8,128)(2,1)S(1)} collective-permute-done((bf16[160,640]{1,0:T(8,128)(2,1)S(1)}, bf16[160,640]{1,0:T(8,128)(2,1)S(1)}, u32[]{:S(2)}, u32[]{:S(2)}) %collective-permute-start.60) | collective-permute-done | bytes 204832 | tf_op jit(solution)/shard_map/ppermute | solution.py:62
  441.9 3.5 collective-permute-done.62
  447.1 2.5 maximum_select_fusion
  (398 shorter events, 139.2 us)
Async XLA Ops:
  5.7 32.2 %collective-permute-start.3 = (bf16[512,1280]{1,0:T(8,128)(2,1)}, bf16[512,1280]{1,0:T(8,128)(2,1)S(1)}, u32[]{:S(2)}, u32[]{:S(2)}) collective-permute-start(bf16[512,1280]{1,0:T(8,128)(2,1)} %pad_maximum_fusion), channel_id=1, source_target_pairs={{0,2},{1,3},{2,0},{3,1},{4,6},{5,7},{6,4},{7,5},{8,10},{9,11},{10,... | collective-permute-start | bytes 3932168 | tf_op jit(solution)/shard_map/ppermute | solution.py:57
  14.0 18.6 %collective-permute-start = (bf16[1,168,640]{2,1,0:T(8,128)(2,1)}, bf16[1,168,640]{2,1,0:T(8,128)(2,1)}, u32[]{:S(2)}, u32[]{:S(2)}) collective-permute-start(bf16[1,168,640]{2,1,0:T(8,128)(2,1)} %bitcast.243), channel_id=1, source_target_pairs={{0,16},{4,20},{8,24},{12,28},{16,0},{20,4},{24,8},{28,12},{1,17},{... | collective-permute-start | bytes 645128 | tf_op jit(solution)/shard_map/ppermute | solution.py:62
  16.6 19.5 %collective-permute-start.1 = (bf16[1,168,640]{2,1,0:T(8,128)(2,1)}, bf16[1,168,640]{2,1,0:T(8,128)(2,1)}, u32[]{:S(2)}, u32[]{:S(2)}) collective-permute-start(bf16[1,168,640]{2,1,0:T(8,128)(2,1)} %bitcast.241), channel_id=1, source_target_pairs={{0,16},{4,20},{8,24},{12,28},{16,0},{20,4},{24,8},{28,12},{1,17},{... | collective-permute-start | bytes 645128 | tf_op jit(solution)/shard_map/ppermute | solution.py:62
  40.7 33.1 %collective-permute-start.5 = (bf16[2,168,640]{2,1,0:T(8,128)(2,1)S(1)}, bf16[2,168,640]{2,1,0:T(8,128)(2,1)S(1)}, u32[]{:S(2)}, u32[]{:S(2)}) collective-permute-start(bf16[2,168,640]{2,1,0:T(8,128)(2,1)S(1)} %constant_dynamic-update-slice_fusion), channel_id=1, source_target_pairs={{0,8},{4,12},{8,0},{12,4},{16,24},{20,28},{24,16},{28,20},{1,9},{5... | collective-permute-start | bytes 1290248 | tf_op jit(solution)/shard_map/ppermute | solution.py:62
  43.5 30.3 %collective-permute-start.6 = (bf16[2,168,640]{2,1,0:T(8,128)(2,1)S(1)}, bf16[2,168,640]{2,1,0:T(8,128)(2,1)S(1)}, u32[]{:S(2)}, u32[]{:S(2)}) collective-permute-start(bf16[2,168,640]{2,1,0:T(8,128)(2,1)S(1)} %constant_dynamic-update-slice_fusion.2), channel_id=1, source_target_pairs={{0,4},{4,0},{8,12},{12,8},{16,20},{20,16},{24,28},{28,24},{1,5},{5... | collective-permute-start | bytes 1290248 | tf_op jit(solution)/shard_map/ppermute | solution.py:62
  45.1 23.8 %collective-permute-start.7 = (bf16[1,160,768]{2,1,0:T(8,128)(2,1)S(1)}, bf16[1,160,768]{2,1,0:T(8,128)(2,1)S(1)}, u32[]{:S(2)}, u32[]{:S(2)}) collective-permute-start(bf16[1,160,768]{2,1,0:T(8,128)(2,1)S(1)} %get-tuple-element.169), channel_id=1, source_target_pairs={{0,16},{4,20},{8,24},{12,28},{16,0},{20,4},{24,8},{28,12},{1,17},{... | collective-permute-start | bytes 737288 | tf_op jit(solution)/shard_map/ppermute | solution.py:62
  47.7 26.1 %collective-permute-start.8 = (bf16[1,160,768]{2,1,0:T(8,128)(2,1)S(1)}, bf16[1,160,768]{2,1,0:T(8,128)(2,1)S(1)}, u32[]{:S(2)}, u32[]{:S(2)}) collective-permute-start(bf16[1,160,768]{2,1,0:T(8,128)(2,1)S(1)} %get-tuple-element.171), channel_id=1, source_target_pairs={{0,16},{4,20},{8,24},{12,28},{16,0},{20,4},{24,8},{28,12},{1,17},{... | collective-permute-start | bytes 737288 | tf_op jit(solution)/shard_map/ppermute | solution.py:62
  49.7 28.8 %collective-permute-start.13 = (bf16[1,160,512]{2,1,0:T(8,128)(2,1)S(1)}, bf16[1,160,512]{2,1,0:T(8,128)(2,1)S(1)}, u32[]{:S(2)}, u32[]{:S(2)}) collective-permute-start(bf16[1,160,512]{2,1,0:T(8,128)(2,1)S(1)} %get-tuple-element.192), channel_id=1, source_target_pairs={{0,16},{4,20},{8,24},{12,28},{16,0},{20,4},{24,8},{28,12},{1,17},{... | collective-permute-start | bytes 491528 | tf_op jit(solution)/shard_map/ppermute | solution.py:62
  73.9 34.0 %collective-permute-start.9 = (bf16[4,168,640]{2,1,0:T(8,128)(2,1)S(1)}, bf16[4,168,640]{2,1,0:T(8,128)(2,1)S(1)}, u32[]{:S(2)}, u32[]{:S(2)}) collective-permute-start(bf16[4,168,640]{2,1,0:T(8,128)(2,1)S(1)} %constant_dynamic-update-slice_fusion.4.refs_1_), channel_id=1, source_target_pairs={{0,4},{4,0},{8,12},{12,8},{16,20},{20,16},{24,28},{28,24},{1,5},{5... | collective-permute-start | bytes 2580488 | tf_op jit(solution)/shard_map/ppermute | solution.py:62
  74.5 33.4 %collective-permute-start.10 = (bf16[4,168,640]{2,1,0:T(8,128)(2,1)S(1)}, bf16[4,168,640]{2,1,0:T(8,128)(2,1)S(1)}, u32[]{:S(2)}, u32[]{:S(2)}) collective-permute-start(bf16[4,168,640]{2,1,0:T(8,128)(2,1)S(1)} %constant_dynamic-update-slice_fusion.6.refs_3_), channel_id=1, source_target_pairs={{0,8},{4,12},{8,0},{12,4},{16,24},{20,28},{24,16},{28,20},{1,9},{5... | collective-permute-start | bytes 2580488 | tf_op jit(solution)/shard_map/ppermute | solution.py:62
  74.7 33.3 %collective-permute-start.11 = (bf16[2,160,768]{2,1,0:T(8,128)(2,1)S(1)}, bf16[2,160,768]{2,1,0:T(8,128)(2,1)S(1)}, u32[]{:S(2)}, u32[]{:S(2)}) collective-permute-start(bf16[2,160,768]{2,1,0:T(8,128)(2,1)S(1)} %constant_dynamic-update-slice_fusion.8), channel_id=1, source_target_pairs={{0,8},{4,12},{8,0},{12,4},{16,24},{20,28},{24,16},{28,20},{1,9},{5... | collective-permute-start | bytes 1474568 | tf_op jit(solution)/shard_map/ppermute | solution.py:62
  76.8 31.2 %collective-permute-start.12 = (bf16[2,160,768]{2,1,0:T(8,128)(2,1)S(1)}, bf16[2,160,768]{2,1,0:T(8,128)(2,1)S(1)}, u32[]{:S(2)}, u32[]{:S(2)}) collective-permute-start(bf16[2,160,768]{2,1,0:T(8,128)(2,1)S(1)} %constant_dynamic-update-slice_fusion.10), channel_id=1, source_target_pairs={{0,4},{4,0},{8,12},{12,8},{16,20},{20,16},{24,28},{28,24},{1,5},{5... | collective-permute-start | bytes 1474568 | tf_op jit(solution)/shard_map/ppermute | solution.py:62
  78.5 24.8 %collective-permute-start.14 = (bf16[1,160,512]{2,1,0:T(8,128)(2,1)S(1)}, bf16[1,160,512]{2,1,0:T(8,128)(2,1)S(1)}, u32[]{:S(2)}, u32[]{:S(2)}) collective-permute-start(bf16[1,160,512]{2,1,0:T(8,128)(2,1)S(1)} %get-tuple-element.194), channel_id=1, source_target_pairs={{0,16},{4,20},{8,24},{12,28},{16,0},{20,4},{24,8},{28,12},{1,17},{... | collective-permute-start | bytes 491528 | tf_op jit(solution)/shard_map/ppermute | solution.py:62
  108.8 22.8 %collective-permute-start.15 = (bf16[1280,1280]{1,0:T(8,128)(2,1)S(1)}, bf16[1280,1280]{1,0:T(8,128)(2,1)}, u32[]{:S(2)}, u32[]{:S(2)}) collective-permute-start(bf16[1280,1280]{1,0:T(8,128)(2,1)S(1)} %bitcast.218), channel_id=1, source_target_pairs={{0,1},{1,0},{2,3},{3,2},{4,5},{5,4},{6,7},{7,6},{8,9},{9,8},{10,11... | collective-permute-start | bytes 9830408 | tf_op jit(solution)/shard_map/ppermute | solution.py:57
  110.7 33.3 %collective-permute-start.16 = (bf16[4,160,768]{2,1,0:T(8,128)(2,1)}, bf16[4,160,768]{2,1,0:T(8,128)(2,1)}, u32[]{:S(2)}, u32[]{:S(2)}) collective-permute-start(bf16[4,160,768]{2,1,0:T(8,128)(2,1)} %constant_dynamic-update-slice_fusion.12.refs_1_), channel_id=1, source_target_pairs={{0,4},{4,0},{8,12},{12,8},{16,20},{20,16},{24,28},{28,24},{1,5},{5... | collective-permute-start | bytes 2949128 | tf_op jit(solution)/shard_map/ppermute | solution.py:62
  112.9 31.1 %collective-permute-start.17 = (bf16[4,160,768]{2,1,0:T(8,128)(2,1)}, bf16[4,160,768]{2,1,0:T(8,128)(2,1)}, u32[]{:S(2)}, u32[]{:S(2)}) collective-permute-start(bf16[4,160,768]{2,1,0:T(8,128)(2,1)} %constant_dynamic-update-slice_fusion.14.refs_3_), channel_id=1, source_target_pairs={{0,8},{4,12},{8,0},{12,4},{16,24},{20,28},{24,16},{28,20},{1,9},{5... | collective-permute-start | bytes 2949128 | tf_op jit(solution)/shard_map/ppermute | solution.py:62
  114.2 29.7 %collective-permute-start.18 = (bf16[2,160,512]{2,1,0:T(8,128)(2,1)}, bf16[2,160,512]{2,1,0:T(8,128)(2,1)}, u32[]{:S(2)}, u32[]{:S(2)}) collective-permute-start(bf16[2,160,512]{2,1,0:T(8,128)(2,1)} %constant_dynamic-update-slice_fusion.16), channel_id=1, source_target_pairs={{0,8},{4,12},{8,0},{12,4},{16,24},{20,28},{24,16},{28,20},{1,9},{5... | collective-permute-start | bytes 983048 | tf_op jit(solution)/shard_map/ppermute | solution.py:62
  117.6 26.4 %collective-permute-start.19 = (bf16[2,160,512]{2,1,0:T(8,128)(2,1)}, bf16[2,160,512]{2,1,0:T(8,128)(2,1)}, u32[]{:S(2)}, u32[]{:S(2)}) collective-permute-start(bf16[2,160,512]{2,1,0:T(8,128)(2,1)} %constant_dynamic-update-slice_fusion.18), channel_id=1, source_target_pairs={{0,4},{4,0},{8,12},{12,8},{16,20},{20,16},{24,28},{28,24},{1,5},{5... | collective-permute-start | bytes 983048 | tf_op jit(solution)/shard_map/ppermute | solution.py:62
  146.3 37.1 %collective-permute-start.24 = (bf16[1280,768]{1,0:T(8,128)(2,1)S(1)}, bf16[1280,768]{1,0:T(8,128)(2,1)S(1)}, u32[]{:S(2)}, u32[]{:S(2)}) collective-permute-start(bf16[1280,768]{1,0:T(8,128)(2,1)S(1)} %bitcast.221), channel_id=1, source_target_pairs={{0,1},{1,0},{2,3},{3,2},{4,5},{5,4},{6,7},{7,6},{8,9},{9,8},{10,11... | collective-permute-start | bytes 5898248 | tf_op jit(solution)/shard_map/ppermute | solution.py:57
  146.4 38.3 %collective-permute-start.25 = (bf16[1280,768]{1,0:T(8,128)(2,1)S(1)}, bf16[1280,768]{1,0:T(8,128)(2,1)}, u32[]{:S(2)}, u32[]{:S(2)}) collective-permute-start(bf16[1280,768]{1,0:T(8,128)(2,1)S(1)} %bitcast.223), channel_id=1, source_target_pairs={{0,1},{1,0},{2,3},{3,2},{4,5},{5,4},{6,7},{7,6},{8,9},{9,8},{10,11... | collective-permute-start | bytes 5898248 | tf_op jit(solution)/shard_map/ppermute | solution.py:57
  153.9 17.7 %collective-permute-start.22 = (bf16[256,1280]{1,0:T(8,128)(2,1)S(1)}, bf16[256,1280]{1,0:T(8,128)(2,1)S(1)}, u32[]{:S(2)}, u32[]{:S(2)}) collective-permute-start(bf16[256,1280]{1,0:T(8,128)(2,1)S(1)} %copy-done.79), channel_id=1, source_target_pairs={{0,2},{1,3},{2,0},{3,1},{4,6},{5,7},{6,4},{7,5},{8,10},{9,11},{10,... | collective-permute-start | bytes 1966088 | tf_op jit(solution)/shard_map/ppermute | solution.py:57
  165.8 17.6 %collective-permute-start.23 = (bf16[256,1280]{1,0:T(8,128)(2,1)S(1)}, bf16[256,1280]{1,0:T(8,128)(2,1)S(1)}, u32[]{:S(2)}, u32[]{:S(2)}) collective-permute-start(bf16[256,1280]{1,0:T(8,128)(2,1)S(1)} %copy-done.78), channel_id=1, source_target_pairs={{0,2},{1,3},{2,0},{3,1},{4,6},{5,7},{6,4},{7,5},{8,10},{9,11},{10,... | collective-permute-start | bytes 1966088 | tf_op jit(solution)/shard_map/ppermute | solution.py:57
  189.4 36.6 %collective-permute-start.26 = (bf16[1280,512]{1,0:T(8,128)(2,1)S(1)}, bf16[1280,512]{1,0:T(8,128)(2,1)}, u32[]{:S(2)}, u32[]{:S(2)}) collective-permute-start(bf16[1280,512]{1,0:T(8,128)(2,1)S(1)} %bitcast.225), channel_id=1, source_target_pairs={{0,1},{1,0},{2,3},{3,2},{4,5},{5,4},{6,7},{7,6},{8,9},{9,8},{10,11... | collective-permute-start | bytes 3932168 | tf_op jit(solution)/shard_map/ppermute | solution.py:57
  189.4 36.5 %collective-permute-start.27 = (bf16[1280,512]{1,0:T(8,128)(2,1)}, bf16[1280,512]{1,0:T(8,128)(2,1)}, u32[]{:S(2)}, u32[]{:S(2)}) collective-permute-start(bf16[1280,512]{1,0:T(8,128)(2,1)} %bitcast.21.refs_5_), channel_id=1, source_target_pairs={{0,1},{1,0},{2,3},{3,2},{4,5},{5,4},{6,7},{7,6},{8,9},{9,8},{10,11... | collective-permute-start | bytes 3932168 | tf_op jit(solution)/shard_map/ppermute | solution.py:57
  224.2 22.0 %collective-permute-start.29 = (bf16[1280,768]{1,0:T(8,128)(2,1)}, bf16[1280,768]{1,0:T(8,128)(2,1)}, u32[]{:S(2)}, u32[]{:S(2)}) collective-permute-start(bf16[1280,768]{1,0:T(8,128)(2,1)} %get-tuple-element.231), channel_id=1, source_target_pairs={{0,1},{1,0},{2,3},{3,2},{4,5},{5,4},{6,7},{7,6},{8,9},{9,8},{10,11... | collective-permute-start | bytes 5898248 | tf_op jit(solution)/shard_map/ppermute | solution.py:57
  224.3 25.0 %collective-permute-start.31 = (bf16[1280,768]{1,0:T(8,128)(2,1)}, bf16[1280,768]{1,0:T(8,128)(2,1)}, u32[]{:S(2)}, u32[]{:S(2)}) collective-permute-start(bf16[1280,768]{1,0:T(8,128)(2,1)} %get-tuple-element.233), channel_id=1, source_target_pairs={{0,1},{1,0},{2,3},{3,2},{4,5},{5,4},{6,7},{7,6},{8,9},{9,8},{10,11... | collective-permute-start | bytes 5898248 | tf_op jit(solution)/shard_map/ppermute | solution.py:57
  248.8 35.0 %collective-permute-start.30 = (bf16[2,2,160,768]{3,2,0,1:T(8,128)(2,1)}, bf16[2,2,160,768]{3,2,0,1:T(8,128)(2,1)}, u32[]{:S(2)}, u32[]{:S(2)}) collective-permute-start(bf16[2,2,160,768]{3,2,0,1:T(8,128)(2,1)} %fusion.11), channel_id=1, source_target_pairs={{0,4},{4,0},{8,12},{12,8},{16,20},{20,16},{24,28},{28,24},{1,5},{5... | collective-permute-start | bytes 2949128 | tf_op jit(solution)/shard_map/ppermute | solution.py:62
  251.8 31.9 %collective-permute-start.32 = (bf16[2,2,160,768]{3,2,0,1:T(8,128)(2,1)}, bf16[2,2,160,768]{3,2,0,1:T(8,128)(2,1)}, u32[]{:S(2)}, u32[]{:S(2)}) collective-permute-start(bf16[2,2,160,768]{3,2,0,1:T(8,128)(2,1)} %fusion.12), channel_id=1, source_target_pairs={{0,8},{4,12},{8,0},{12,4},{16,24},{20,28},{24,16},{28,20},{1,9},{5... | collective-permute-start | bytes 2949128 | tf_op jit(solution)/shard_map/ppermute | solution.py:62
  253.3 17.9 %collective-permute-start.33 = (bf16[256,1280]{1,0:T(8,128)(2,1)}, bf16[256,1280]{1,0:T(8,128)(2,1)S(1)}, u32[]{:S(2)}, u32[]{:S(2)}) collective-permute-start(bf16[256,1280]{1,0:T(8,128)(2,1)} %get-tuple-element.234), channel_id=1, source_target_pairs={{0,2},{1,3},{2,0},{3,1},{4,6},{5,7},{6,4},{7,5},{8,10},{9,11},{10,... | collective-permute-start | bytes 1966088 | tf_op jit(solution)/shard_map/ppermute | solution.py:57
  254.8 28.9 %collective-permute-start.34 = (bf16[256,1280]{1,0:T(8,128)(2,1)S(1)}, bf16[256,1280]{1,0:T(8,128)(2,1)S(1)}, u32[]{:S(2)}, u32[]{:S(2)}) collective-permute-start(bf16[256,1280]{1,0:T(8,128)(2,1)S(1)} %copy-done.76), channel_id=1, source_target_pairs={{0,2},{1,3},{2,0},{3,1},{4,6},{5,7},{6,4},{7,5},{8,10},{9,11},{10,... | collective-permute-start | bytes 1966088 | tf_op jit(solution)/shard_map/ppermute | solution.py:57
  260.4 52.5 %collective-permute-start.38 = (bf16[2,2,160,512]{3,2,0,1:T(8,128)(2,1)S(1)}, bf16[2,2,160,512]{3,2,0,1:T(8,128)(2,1)S(1)}, u32[]{:S(2)}, u32[]{:S(2)}) collective-permute-start(bf16[2,2,160,512]{3,2,0,1:T(8,128)(2,1)S(1)} %fusion.19), channel_id=1, source_target_pairs={{0,4},{4,0},{8,12},{12,8},{16,20},{20,16},{24,28},{28,24},{1,5},{5... | collective-permute-start | bytes 1966088 | tf_op jit(solution)/shard_map/ppermute | solution.py:62
  271.2 41.8 %collective-permute-start.39 = (bf16[2,2,160,512]{3,2,0,1:T(8,128)(2,1)S(1)}, bf16[2,2,160,512]{3,2,0,1:T(8,128)(2,1)S(1)}, u32[]{:S(2)}, u32[]{:S(2)}) collective-permute-start(bf16[2,2,160,512]{3,2,0,1:T(8,128)(2,1)S(1)} %fusion.20), channel_id=1, source_target_pairs={{0,8},{4,12},{8,0},{12,4},{16,24},{20,28},{24,16},{28,20},{1,9},{5... | collective-permute-start | bytes 1966088 | tf_op jit(solution)/shard_map/ppermute | solution.py:62
  286.4 27.4 %collective-permute-start.36 = (bf16[2,160,768]{2,1,0:T(8,128)(2,1)S(1)}, bf16[2,160,768]{2,1,0:T(8,128)(2,1)S(1)}, u32[]{:S(2)}, u32[]{:S(2)}) collective-permute-start(bf16[2,160,768]{2,1,0:T(8,128)(2,1)S(1)} %get-tuple-element.308), channel_id=1, source_target_pairs={{0,8},{4,12},{8,0},{12,4},{16,24},{20,28},{24,16},{28,20},{1,9},{5... | collective-permute-start | bytes 1474568 | tf_op jit(solution)/shard_map/ppermute | solution.py:62
  286.9 28.5 %collective-permute-start.40 = (bf16[256,1280]{1,0:T(8,128)(2,1)}, bf16[256,1280]{1,0:T(8,128)(2,1)}, u32[]{:S(2)}, u32[]{:S(2)}) collective-permute-start(bf16[256,1280]{1,0:T(8,128)(2,1)} %get-tuple-element.251), channel_id=1, source_target_pairs={{0,2},{1,3},{2,0},{3,1},{4,6},{5,7},{6,4},{7,5},{8,10},{9,11},{10,... | collective-permute-start | bytes 1966088 | tf_op jit(solution)/shard_map/ppermute | solution.py:57
  291.0 23.6 %collective-permute-start.37 = (bf16[2,160,768]{2,1,0:T(8,128)(2,1)S(1)}, bf16[2,160,768]{2,1,0:T(8,128)(2,1)S(1)}, u32[]{:S(2)}, u32[]{:S(2)}) collective-permute-start(bf16[2,160,768]{2,1,0:T(8,128)(2,1)S(1)} %get-tuple-element.306), channel_id=1, source_target_pairs={{0,4},{4,0},{8,12},{12,8},{16,20},{20,16},{24,28},{28,24},{1,5},{5... | collective-permute-start | bytes 1474568 | tf_op jit(solution)/shard_map/ppermute | solution.py:62
  316.3 48.4 %collective-permute-start.45 = (bf16[1280,640]{1,0:T(8,128)(2,1)}, bf16[1280,640]{1,0:T(8,128)(2,1)}, u32[]{:S(2)}, u32[]{:S(2)}) collective-permute-start(bf16[1280,640]{1,0:T(8,128)(2,1)} %get-tuple-element.265), channel_id=1, source_target_pairs={{0,1},{1,0},{2,3},{3,2},{4,5},{5,4},{6,7},{7,6},{8,9},{9,8},{10,11... | collective-permute-start | bytes 4915208 | tf_op jit(solution)/shard_map/ppermute | solution.py:57
  316.3 48.4 %collective-permute-start.46 = (bf16[1280,640]{1,0:T(8,128)(2,1)}, bf16[1280,640]{1,0:T(8,128)(2,1)}, u32[]{:S(2)}, u32[]{:S(2)}) collective-permute-start(bf16[1280,640]{1,0:T(8,128)(2,1)} %get-tuple-element.266), channel_id=1, source_target_pairs={{0,1},{1,0},{2,3},{3,2},{4,5},{5,4},{6,7},{7,6},{8,9},{9,8},{10,11... | collective-permute-start | bytes 4915208 | tf_op jit(solution)/shard_map/ppermute | solution.py:57
  322.0 20.3 %collective-permute-start.41 = (bf16[160,768]{1,0:T(8,128)(2,1)S(1)}, bf16[160,768]{1,0:T(8,128)(2,1)S(1)}, u32[]{:S(2)}, u32[]{:S(2)}) collective-permute-start(bf16[160,768]{1,0:T(8,128)(2,1)S(1)} %fusion.35), channel_id=1, source_target_pairs={{0,16},{4,20},{8,24},{12,28},{16,0},{20,4},{24,8},{28,12},{1,17},{... | collective-permute-start | bytes 737288 | tf_op jit(solution)/shard_map/ppermute | solution.py:62
  325.3 39.4 %collective-permute-start.42 = (bf16[160,768]{1,0:T(8,128)(2,1)}, bf16[160,768]{1,0:T(8,128)(2,1)}, u32[]{:S(2)}, u32[]{:S(2)}) collective-permute-start(bf16[160,768]{1,0:T(8,128)(2,1)} %fusion.36), channel_id=1, source_target_pairs={{0,16},{4,20},{8,24},{12,28},{16,0},{20,4},{24,8},{28,12},{1,17},{... | collective-permute-start | bytes 737288 | tf_op jit(solution)/shard_map/ppermute | solution.py:62
  326.9 37.8 %collective-permute-start.43 = (bf16[2,160,512]{2,1,0:T(8,128)(2,1)}, bf16[2,160,512]{2,1,0:T(8,128)(2,1)}, u32[]{:S(2)}, u32[]{:S(2)}) collective-permute-start(bf16[2,160,512]{2,1,0:T(8,128)(2,1)} %get-tuple-element.315), channel_id=1, source_target_pairs={{0,8},{4,12},{8,0},{12,4},{16,24},{20,28},{24,16},{28,20},{1,9},{5... | collective-permute-start | bytes 983048 | tf_op jit(solution)/shard_map/ppermute | solution.py:62
  342.3 22.4 %collective-permute-start.44 = (bf16[2,160,512]{2,1,0:T(8,128)(2,1)}, bf16[2,160,512]{2,1,0:T(8,128)(2,1)}, u32[]{:S(2)}, u32[]{:S(2)}) collective-permute-start(bf16[2,160,512]{2,1,0:T(8,128)(2,1)} %get-tuple-element.314), channel_id=1, source_target_pairs={{0,4},{4,0},{8,12},{12,8},{16,20},{20,16},{24,28},{28,24},{1,5},{5... | collective-permute-start | bytes 983048 | tf_op jit(solution)/shard_map/ppermute | solution.py:62
  367.5 24.4 %collective-permute-start.49 = (bf16[2,2,160,640]{3,2,0,1:T(8,128)(2,1)S(1)}, bf16[2,2,160,640]{3,2,0,1:T(8,128)(2,1)S(1)}, u32[]{:S(2)}, u32[]{:S(2)}) collective-permute-start(bf16[2,2,160,640]{3,2,0,1:T(8,128)(2,1)S(1)} %fusion.15), channel_id=1, source_target_pairs={{0,4},{4,0},{8,12},{12,8},{16,20},{20,16},{24,28},{28,24},{1,5},{5... | collective-permute-start | bytes 2457608 | tf_op jit(solution)/shard_map/ppermute | solution.py:62
  370.4 24.7 %collective-permute-start.50 = (bf16[2,2,160,640]{3,2,0,1:T(8,128)(2,1)S(1)}, bf16[2,2,160,640]{3,2,0,1:T(8,128)(2,1)S(1)}, u32[]{:S(2)}, u32[]{:S(2)}) collective-permute-start(bf16[2,2,160,640]{3,2,0,1:T(8,128)(2,1)S(1)} %fusion.16), channel_id=1, source_target_pairs={{0,8},{4,12},{8,0},{12,4},{16,24},{20,28},{24,16},{28,20},{1,9},{5... | collective-permute-start | bytes 2457608 | tf_op jit(solution)/shard_map/ppermute | solution.py:62
  374.4 17.6 %collective-permute-start.48 = (bf16[160,512]{1,0:T(8,128)(2,1)S(1)}, bf16[160,512]{1,0:T(8,128)(2,1)S(1)}, u32[]{:S(2)}, u32[]{:S(2)}) collective-permute-start(bf16[160,512]{1,0:T(8,128)(2,1)S(1)} %fusion.40), channel_id=1, source_target_pairs={{0,16},{4,20},{8,24},{12,28},{16,0},{20,4},{24,8},{28,12},{1,17},{... | collective-permute-start | bytes 491528 | tf_op jit(solution)/shard_map/ppermute | solution.py:62
  398.2 30.6 %collective-permute-start.52 = (bf16[128,1280]{1,0:T(8,128)(2,1)}, bf16[128,1280]{1,0:T(8,128)(2,1)}, u32[]{:S(2)}, u32[]{:S(2)}) collective-permute-start(bf16[128,1280]{1,0:T(8,128)(2,1)} %get-tuple-element.324), channel_id=1, source_target_pairs={{0,1},{1,0},{2,3},{3,2},{4,5},{5,4},{6,7},{7,6},{8,9},{9,8},{10,11... | collective-permute-start | bytes 983048 | tf_op jit(solution)/shard_map/ppermute | solution.py:57
  401.2 45.9 %collective-permute-start.53 = (f32[128,1280]{1,0:T(8,128)}, f32[128,1280]{1,0:T(8,128)}, u32[]{:S(2)}, u32[]{:S(2)}) collective-permute-start(f32[128,1280]{1,0:T(8,128)} %get-tuple-element.318), channel_id=1, source_target_pairs={{0,1},{1,0},{2,3},{3,2},{4,5},{5,4},{6,7},{7,6},{8,9},{9,8},{10,11... | collective-permute-start | bytes 1966088 | tf_op jit(solution)/shard_map/ppermute | solution.py:57
  403.4 23.8 %collective-permute-start.59 = (bf16[2,160,640]{2,1,0:T(8,128)(2,1)S(1)}, bf16[2,160,640]{2,1,0:T(8,128)(2,1)S(1)}, u32[]{:S(2)}, u32[]{:S(2)}) collective-permute-start(bf16[2,160,640]{2,1,0:T(8,128)(2,1)S(1)} %get-tuple-element.311), channel_id=1, source_target_pairs={{0,8},{4,12},{8,0},{12,4},{16,24},{20,28},{24,16},{28,20},{1,9},{5... | collective-permute-start | bytes 1228808 | tf_op jit(solution)/shard_map/ppermute | solution.py:62
  403.6 27.2 %collective-permute-start.61 = (bf16[2,160,640]{2,1,0:T(8,128)(2,1)S(1)}, bf16[2,160,640]{2,1,0:T(8,128)(2,1)S(1)}, u32[]{:S(2)}, u32[]{:S(2)}) collective-permute-start(bf16[2,160,640]{2,1,0:T(8,128)(2,1)S(1)} %get-tuple-element.309), channel_id=1, source_target_pairs={{0,4},{4,0},{8,12},{12,8},{16,20},{20,16},{24,28},{28,24},{1,5},{5... | collective-permute-start | bytes 1228808 | tf_op jit(solution)/shard_map/ppermute | solution.py:62
  (102 other events, 729.7 us)
